TPU v7x, 32 devices: a whole 2x2x4 slice. The times are simulated.
32 devices in a mesh: dp: 8 (over y, x, core), tensor: 4 (over z).
Axes of the slice: x: 2, y: 2, z: 4, core: 2. Of those that a mesh axis runs over, the one named last changes fastest.
Arguments:
- hidden_in: bfloat16 [8, 1024, 1024], P('dp', 'tensor'), may hold values from -40 to 40
- segment_ids: int32 [8, 1024], P('dp'), may hold values from 0 to 1024, as said below
- gain_attn: float32 [1024], replicated, may hold values from 0.25 to 1.75
- gain_mlp: float32 [1024], replicated, may hold values from 0.25 to 1.75
- w_qkv: bfloat16 [1024, 3, 1024], P(None, None, 'tensor'), may hold values from -3 to 3
- w_out: bfloat16 [1024, 1024], P('tensor'), may hold values from -0.75 to 0.75
- w_in: bfloat16 [1024, 2, 2624], P(None, None, 'tensor'), may hold values from -0.1875 to 0.1875
- w_down: bfloat16 [2624, 1024], P('tensor'), may hold values from -0.125 to 0.125
- out_grad: bfloat16 [8, 1024, 1024], P('dp', 'tensor'), may hold values from -24 to 24
Outputs:
- hidden_out: bfloat16 [8, 1024, 1024], P('dp', 'tensor')
- hidden_grad: float32 [8, 1024, 1024], P('dp', 'tensor')
- gain_attn_grad: float32 [1024], P('tensor')
- gain_mlp_grad: float32 [1024], P('tensor')
- w_qkv_grad: float32 [1024, 3, 1024], P(None, None, 'tensor')
- w_out_grad: float32 [1024, 1024], P('tensor')
- w_in_grad: float32 [1024, 2, 2624], P(None, None, 'tensor')
- w_down_grad: float32 [2624, 1024], P('tensor')
Inputs may be any that keep to these rules, and one draw needn't show every extreme that they name: `segment_ids`: within a group the ids never fall along the slots; documents carry ids 0, 1, 2 and so on in order; the id 1024 marks padding, which fills the last slots of every group, one or more of them.
All inputs are finite; a program needn't handle non-finite values.
Results may differ from a plain program's by a relative error of at most 0.035.
Values may be sent and summed in bfloat16 or wider, within the bound.
A program may use at most 128 MiB of HBM per device.

v0:
```python
import math

import jax
import jax.numpy as jnp
from jax import lax
from jax.sharding import PartitionSpec as P

HEAD_DIM = 64


eps_norm = 1e-05
rope_theta = 160000.0
neg_fill = -1e30
sqrt_half = 0.7071067811865476
inv_sqrt_two_pi = 0.3989422804014327


def norm_fwd(rows_f, gain_vec):
    mean_row = jnp.mean(rows_f, axis=-1, keepdims=True)
    centred = rows_f - mean_row
    var_row = jnp.mean(centred * centred, axis=-1, keepdims=True)
    inv_std = lax.rsqrt(var_row + eps_norm)
    hat_rows = centred * inv_std
    return ((hat_rows * gain_vec).astype(jnp.bfloat16), hat_rows, inv_std)


def norm_bwd(grad_norm, hat_rows, inv_std, gain_vec):
    grad_hat = grad_norm * gain_vec
    mean_one = jnp.mean(grad_hat, axis=-1, keepdims=True)
    mean_two = jnp.mean(grad_hat * hat_rows, axis=-1, keepdims=True)
    return inv_std * (grad_hat - mean_one - hat_rows * mean_two)


def half_turn(field_in):
    half_dim = field_in.shape[-1] // 2
    return jnp.concatenate([-field_in[..., half_dim:], field_in[..., :half_dim]], axis=-1)


def positions_of(seg_row):
    before = jnp.sum((seg_row[None, :] < seg_row[:, None]).astype(jnp.int32), axis=1)
    return jnp.arange(seg_row.shape[0], dtype=jnp.int32) - before


def rope_tables(positions, head_dim):
    half_dim = head_dim // 2
    inv_freq = jnp.exp(
        jnp.arange(half_dim, dtype=jnp.float32) * (-2.0 * math.log(rope_theta) / head_dim)
    )
    angles = positions.astype(jnp.float32)[:, None] * inv_freq[None, :]
    cos_tab = jnp.concatenate([jnp.cos(angles), jnp.cos(angles)], axis=-1)
    sin_tab = jnp.concatenate([jnp.sin(angles), jnp.sin(angles)], axis=-1)
    return (cos_tab[:, None, :], sin_tab[:, None, :])


def rope_apply(field_in, cos_tab, sin_tab):
    return field_in * cos_tab + half_turn(field_in) * sin_tab


def rope_back(grad_in, cos_tab, sin_tab):
    return grad_in * cos_tab - half_turn(grad_in * sin_tab)


def gelu_val(field_in):
    return 0.5 * field_in * (1.0 + lax.erf(field_in * sqrt_half))


def gelu_slope(field_in):
    return (
        0.5 * (1.0 + lax.erf(field_in * sqrt_half))
        + field_in * jnp.exp(-0.5 * field_in * field_in) * inv_sqrt_two_pi
    )


def attend_fwd(queries, key_rows, value_rows, seg_row):
    total_rows = queries.shape[0]
    block_rows = min(512, total_rows)
    scale_val = 1.0 / math.sqrt(queries.shape[2])

    def one_block(block_idx):
        start_row = block_idx * block_rows
        query_blk = lax.dynamic_slice_in_dim(queries, start_row, block_rows, 0)
        seg_blk = lax.dynamic_slice_in_dim(seg_row, start_row, block_rows, 0)
        scores = (
            jnp.einsum("qhd,khd->hqk", query_blk, key_rows, preferred_element_type=jnp.float32)
            * scale_val
        )
        same_doc = seg_blk[:, None] == seg_row[None, :]
        scores = jnp.where(same_doc[None], scores, neg_fill)
        row_top = jnp.max(scores, axis=-1, keepdims=True)
        exp_vals = jnp.exp(scores - row_top)
        row_total = jnp.sum(exp_vals, axis=-1, keepdims=True)
        prob_bf = (exp_vals / row_total).astype(jnp.bfloat16)
        out_blk = jnp.einsum(
            "hqk,khd->qhd", prob_bf, value_rows, preferred_element_type=jnp.float32
        ).astype(jnp.bfloat16)
        return (out_blk, (row_top + jnp.log(row_total))[..., 0])

    out_blocks, lse_blocks = lax.map(
        one_block, jnp.arange(total_rows // block_rows, dtype=jnp.int32)
    )
    head_count = queries.shape[1]
    att_out = out_blocks.reshape(total_rows, head_count, queries.shape[2])
    lse_rows = jnp.transpose(lse_blocks, (1, 0, 2)).reshape(head_count, total_rows)
    return (att_out, lse_rows)


def attend_bwd(queries, key_rows, value_rows, seg_row, att_out, grad_att, lse_rows):
    total_rows = queries.shape[0]
    block_rows = min(512, total_rows)
    scale_val = 1.0 / math.sqrt(queries.shape[2])
    delta_rows = jnp.sum(grad_att.astype(jnp.float32) * att_out.astype(jnp.float32), axis=-1)

    def one_block(acc_pair, block_idx):
        grad_key, grad_value = acc_pair
        start_row = block_idx * block_rows
        query_blk = lax.dynamic_slice_in_dim(queries, start_row, block_rows, 0)
        grad_blk = lax.dynamic_slice_in_dim(grad_att, start_row, block_rows, 0)
        seg_blk = lax.dynamic_slice_in_dim(seg_row, start_row, block_rows, 0)
        delta_blk = lax.dynamic_slice_in_dim(delta_rows, start_row, block_rows, 0)
        lse_blk = lax.dynamic_slice_in_dim(lse_rows, start_row, block_rows, 1)
        scores = (
            jnp.einsum("qhd,khd->hqk", query_blk, key_rows, preferred_element_type=jnp.float32)
            * scale_val
        )
        same_doc = seg_blk[:, None] == seg_row[None, :]
        scores = jnp.where(same_doc[None], scores, neg_fill)
        prob_f = jnp.exp(scores - lse_blk[:, :, None])
        grad_prob = jnp.einsum(
            "qhd,khd->hqk", grad_blk, value_rows, preferred_element_type=jnp.float32
        )
        grad_score = prob_f * (grad_prob - jnp.transpose(delta_blk)[:, :, None])
        prob_bf = prob_f.astype(jnp.bfloat16)
        score_bf = grad_score.astype(jnp.bfloat16)
        grad_value = grad_value + jnp.einsum(
            "hqk,qhd->khd", prob_bf, grad_blk, preferred_element_type=jnp.float32
        )
        grad_key = (
            grad_key
            + jnp.einsum("hqk,qhd->khd", score_bf, query_blk, preferred_element_type=jnp.float32)
            * scale_val
        )
        grad_query_blk = (
            jnp.einsum("hqk,khd->qhd", score_bf, key_rows, preferred_element_type=jnp.float32)
            * scale_val
        )
        return ((grad_key, grad_value), grad_query_blk)

    zero_rows = jnp.zeros(key_rows.shape, jnp.float32)
    acc_pair, query_blocks = lax.scan(
        one_block, (zero_rows, zero_rows), jnp.arange(total_rows // block_rows, dtype=jnp.int32)
    )
    return (query_blocks.reshape(queries.shape), acc_pair[0], acc_pair[1])


def shards(hidden_in, segment_ids, gain_attn, gain_mlp, w_qkv, w_out, w_in, w_down, out_grad):
    n_parts = lax.axis_size("tensor")
    shard_rows = hidden_in.shape[1]
    total_rows = shard_rows * n_parts
    model_width = hidden_in.shape[2]
    width_local = w_qkv.shape[2]
    head_local = width_local // HEAD_DIM
    ff_local = w_in.shape[2]
    my_index = lax.axis_index("tensor")
    seg_row = segment_ids[0]
    positions = positions_of(seg_row)
    cos_tab, sin_tab = rope_tables(positions, HEAD_DIM)
    my_seg = lax.dynamic_slice_in_dim(seg_row, my_index * shard_rows, shard_rows, 0)
    valid_rows = (my_seg < total_rows).astype(jnp.float32)
    rows_f = hidden_in[0].astype(jnp.float32)
    normed_attn, hat_attn, inv_attn = norm_fwd(rows_f, gain_attn)
    gathered_attn = lax.all_gather(normed_attn, "tensor", axis=0, tiled=True)
    projected = jnp.dot(
        gathered_attn,
        w_qkv.reshape(model_width, 3 * width_local),
        preferred_element_type=jnp.float32,
    )
    projected = projected.reshape(total_rows, 3, head_local, HEAD_DIM)
    queries = rope_apply(projected[:, 0], cos_tab, sin_tab).astype(jnp.bfloat16)
    key_rows = rope_apply(projected[:, 1], cos_tab, sin_tab).astype(jnp.bfloat16)
    value_rows = projected[:, 2].astype(jnp.bfloat16)
    att_out, lse_rows = attend_fwd(queries, key_rows, value_rows, seg_row)
    att_flat = att_out.reshape(total_rows, width_local)
    rows_blk = att_flat
    att_sum = lax.psum_scatter(
        jnp.dot(rows_blk, w_out, preferred_element_type=jnp.float32).astype(jnp.bfloat16),
        "tensor",
        scatter_dimension=0,
        tiled=True,
    ).astype(jnp.float32)
    mid_rows = rows_f + att_sum
    normed_mlp, hat_mlp, inv_mlp = norm_fwd(mid_rows, gain_mlp)
    gathered_mlp = lax.all_gather(normed_mlp, "tensor", axis=0, tiled=True)
    pre_act = jnp.dot(
        gathered_mlp, w_in.reshape(model_width, 2 * ff_local), preferred_element_type=jnp.float32
    )
    pre_act = pre_act.reshape(total_rows, 2, ff_local)
    up_part = pre_act[:, 0]
    gate_part = pre_act[:, 1]
    act_up = gelu_val(up_part)
    mixed_act = (act_up * gate_part).astype(jnp.bfloat16)
    rows_blk = mixed_act
    mlp_sum = lax.psum_scatter(
        jnp.dot(rows_blk, w_down, preferred_element_type=jnp.float32).astype(jnp.bfloat16),
        "tensor",
        scatter_dimension=0,
        tiled=True,
    ).astype(jnp.float32)
    final_rows = (mid_rows + mlp_sum).astype(jnp.bfloat16)
    grad_top = out_grad[0].astype(jnp.float32) * valid_rows[:, None]
    grad_all = lax.all_gather(grad_top.astype(jnp.bfloat16), "tensor", axis=0, tiled=True)
    grad_down = lax.dot_general(
        mixed_act, grad_all, (((0,), (0,)), ((), ())), preferred_element_type=jnp.float32
    )
    d_mixed = lax.dot_general(
        grad_all, w_down, (((1,), (1,)), ((), ())), preferred_element_type=jnp.float32
    )
    d_up = d_mixed * gate_part * gelu_slope(up_part)
    d_gate = d_mixed * act_up
    d_pre = jnp.stack([d_up, d_gate], axis=1).astype(jnp.bfloat16)
    grad_in = lax.dot_general(
        gathered_mlp, d_pre, (((0,), (0,)), ((), ())), preferred_element_type=jnp.float32
    )
    rows_blk = d_pre
    d_norm_mlp = lax.psum_scatter(
        lax.dot_general(
            rows_blk, w_in, (((1, 2), (1, 2)), ((), ())), preferred_element_type=jnp.float32
        ).astype(jnp.bfloat16),
        "tensor",
        scatter_dimension=0,
        tiled=True,
    ).astype(jnp.float32)
    gain_mlp_part = jnp.sum(d_norm_mlp * hat_mlp, axis=0)
    d_mid = grad_top + norm_bwd(d_norm_mlp, hat_mlp, inv_mlp, gain_mlp)
    d_mid_all = lax.all_gather(d_mid.astype(jnp.bfloat16), "tensor", axis=0, tiled=True)
    grad_out_w = lax.dot_general(
        att_flat, d_mid_all, (((0,), (0,)), ((), ())), preferred_element_type=jnp.float32
    )
    d_att = lax.dot_general(
        d_mid_all, w_out, (((1,), (1,)), ((), ())), preferred_element_type=jnp.float32
    )
    d_att = d_att.astype(jnp.bfloat16).reshape(total_rows, head_local, HEAD_DIM)
    grad_query, grad_key, grad_value = attend_bwd(
        queries, key_rows, value_rows, seg_row, att_out, d_att, lse_rows
    )
    grad_query = rope_back(grad_query, cos_tab, sin_tab)
    grad_key = rope_back(grad_key, cos_tab, sin_tab)
    d_proj = (
        jnp.stack([grad_query, grad_key, grad_value], axis=1)
        .reshape(total_rows, 3, width_local)
        .astype(jnp.bfloat16)
    )
    grad_qkv = lax.dot_general(
        gathered_attn, d_proj, (((0,), (0,)), ((), ())), preferred_element_type=jnp.float32
    )
    rows_blk = d_proj
    d_norm_attn = lax.psum_scatter(
        lax.dot_general(
            rows_blk, w_qkv, (((1, 2), (1, 2)), ((), ())), preferred_element_type=jnp.float32
        ).astype(jnp.bfloat16),
        "tensor",
        scatter_dimension=0,
        tiled=True,
    ).astype(jnp.float32)
    gain_attn_part = jnp.sum(d_norm_attn * hat_attn, axis=0)
    d_rows = d_mid + norm_bwd(d_norm_attn, hat_attn, inv_attn, gain_attn)
    gain_both = lax.psum_scatter(
        jnp.stack([gain_attn_part, gain_mlp_part]), "tensor", scatter_dimension=1, tiled=True
    )
    grad_qkv, grad_out_w, grad_in, grad_down, gain_both = lax.psum(
        (grad_qkv, grad_out_w, grad_in, grad_down, gain_both), "dp"
    )
    return (
        final_rows[None],
        d_rows[None],
        gain_both[0],
        gain_both[1],
        grad_qkv,
        grad_out_w,
        grad_in,
        grad_down,
    )


def solution(mesh):
    return jax.shard_map(
        shards,
        mesh=mesh,
        in_specs=(
            P("dp", "tensor", None),
            P("dp", None),
            P(),
            P(),
            P(None, None, "tensor"),
            P("tensor", None),
            P(None, None, "tensor"),
            P("tensor", None),
            P("dp", "tensor", None),
        ),
        out_specs=(
            P("dp", "tensor", None),
            P("dp", "tensor", None),
            P("tensor"),
            P("tensor"),
            P(None, None, "tensor"),
            P("tensor", None),
            P(None, None, "tensor"),
            P("tensor", None),
        ),
        check_vma=False,
    )
```

profile of v0, /device:TPU:0, one launch (start us, length us, event | category | flops | bytes accessed | tf_op | source)
XLA Modules:
  0.0 687.8 jit_solution(1300164859331392286)
XLA Ops:
  17.2 44.0 %all-gather.5.cloned.1.call-done = bf16[1024,1024]{1,0:T(8,128)(2,1)} async-done(((bf16[256,1024]{1,0:T(8,128)(2,1)}), bf16[1024,1024]{1,0:T(8,128)(2,1)}) %all-gather.5.cloned.1.call-update) | async-done | bytes 2097168 | tf_op jit(solution)/shard_map/all_gather | solution.py:171
  61.2 3.9 fusion.44
  68.4 21.1 %while.27 = (s32[]{:T(128)}, bf16[2,512,4,64]{1,3,2,0:T(8,128)(2,1)}, f32[2,4,512]{2,1,0:T(4,128)S(1)}, s32[2]{0:T(128)S(1)}, s32[1024]{0:T(1024)S(1)}, /*index=...) while((s32[]{:T(128)}, ...), condition=%wide.region_6.7_spmd, body=%wide.region_3.6_spmd.sunk | while | flops 562690048 | bytes 35203364 | solution.py:98
  95.2 42.5 %reduce-scatter.8.cloned.1.call-done = bf16[256,1024]{1,0:T(8,128)(2,1)} async-done(((bf16[1024,1024]{1,0:T(8,128)(2,1)}), bf16[256,1024]{1,0:T(8,128)(2,1)}) %reduce-scatter.8.cloned.1.call-update) | async-done | bytes 524304 | tf_op jit(solution)/shard_map/reduce_scatter | solution.py:184
  145.2 42.7 %all-gather.7.cloned.1.call-done = bf16[1024,1024]{1,0:T(8,128)(2,1)} async-done(((bf16[256,1024]{1,0:T(8,128)(2,1)}), bf16[1024,1024]{1,0:T(8,128)(2,1)}) %all-gather.7.cloned.1.call-update) | async-done | bytes 2097168 | tf_op jit(solution)/shard_map/all_gather | solution.py:192
  187.9 6.3 fusion.42
  194.2 40.2 %all-gather.9.cloned.1.call-done = bf16[1024,1024]{1,0:T(8,128)(2,1)} async-done(((bf16[256,1024]{1,0:T(8,128)(2,1)}), bf16[1024,1024]{1,0:T(8,128)(2,1)}) %all-gather.9.cloned.1.call-update) | async-done | bytes 2097168 | tf_op jit(solution)/shard_map/all_gather | solution.py:210
  234.4 7.5 %fusion.52 = (bf16[1024,1,656]{0,2,1:T(8,128)(2,1)S(1)}, bf16[1024,1,656]{0,2,1:T(8,128)(2,1)S(1)}, bf16[1024,656]{0,1:T(8,128)(2,1)}) fusion(f32[1024,2,656]{0,2,1:T(8,128)} %fusion.42, bf16[1024,1024]{1,0:T(8,128)(2,1)} %all-gather.9.cloned.1.call-done, bf16[656,1024]{1,0:T(8,128)(2,1)} %param.20), kind=kOutput, calls=%fused_computation.73 | convolution fusion | flops 1387151360 | bytes 12845056 | tf_op jit(solution)/shard_map/dot_general | solution.py:214
  243.4 4.6 bitcast_convert_fusion.1
  248.1 5.0 convolution_convert_fusion.1
  253.2 37.5 %reduce-scatter.12.cloned.1.call-done = bf16[256,1024]{1,0:T(8,128)(2,1)} async-done(((bf16[1024,1024]{1,0:T(8,128)(2,1)}), bf16[256,1024]{1,0:T(8,128)(2,1)}) %reduce-scatter.12.cloned.1.call-update) | async-done | bytes 524304 | tf_op jit(solution)/shard_map/reduce_scatter | solution.py:224
  292.3 43.9 %reduce-scatter.10.cloned.1.call-done = bf16[256,1024]{1,0:T(8,128)(2,1)} async-done(((bf16[1024,1024]{1,0:T(8,128)(2,1)}), bf16[256,1024]{1,0:T(8,128)(2,1)}) %reduce-scatter.10.cloned.1.call-update) | async-done | bytes 524304 | tf_op jit(solution)/shard_map/reduce_scatter | solution.py:202
  343.2 41.2 %all-gather.11.cloned.1.call-done = bf16[1024,1024]{1,0:T(8,128)(2,1)} async-done(((bf16[256,1024]{1,0:T(8,128)(2,1)}), bf16[1024,1024]{1,0:T(8,128)(2,1)}) %all-gather.11.cloned.1.call-update) | async-done | bytes 2097168 | tf_op jit(solution)/shard_map/all_gather | solution.py:234
  384.4 3.6 multiply_reduce_fusion
  388.0 25.4 %while.28 = (s32[]{:T(128)}, f32[1024,4,64]{0,2,1:T(8,128)S(1)}, f32[1024,4,64]{0,2,1:T(8,128)}, f32[2,512,4,64]{1,3,2,0:T(8,128)}, s32[2]{0:T(128)S(1)}, /*inde...) while((s32[]{:T(128)}, f32[1024,4,64]{0,2,1:T(8,128)S(1)}, ...), condition=%wide.region_16.17_spmd.clone, body=%wide.region_15.16_spmd.clone.sunk | while | flops 1365114880 | bytes 67701168 | solution.py:149
  406.5 3.3 multiply_convert_fusion.5
  431.0 4.5 fusion.96
  435.6 4.7 fusion.48
  440.4 3.5 fusion.46
  443.9 29.4 %reduce-scatter.14.cloned.1.call-done = bf16[256,1024]{1,0:T(8,128)(2,1)} async-done(((bf16[1024,1024]{1,0:T(8,128)(2,1)}), bf16[256,1024]{1,0:T(8,128)(2,1)}) %reduce-scatter.14.cloned.1.call-update) | async-done | bytes 524304 | tf_op jit(solution)/shard_map/reduce_scatter | solution.py:256
  482.1 15.1 %reduce-scatter.16.cloned.1.call-done = f32[256,2]{1,0:T(8,128)} async-done(((f32[1024,2]{1,0:T(8,128)}), f32[256,2]{1,0:T(8,128)}) %reduce-scatter.16.cloned.1.call-update) | async-done | bytes 2064
  498.1 12.3 %psum.35 = f32[2,256]{1,0:T(2,128)S(1)} all-reduce(f32[2,256]{1,0:T(2,128)S(1)} %copy.63), channel_id=1, replica_groups=mesh['dp'=8,'tensor'=4] {'dp'}, use_global_device_ids=true, to_apply=%region_23.24 | all-reduce | flops 512 | bytes 4096 | tf_op jit(solution)/shard_map/psum | solution.py:269
  511.0 158.0 %all-reduce.3.cloned.1.call-done = (f32[1024,3,256]{2,0,1:T(8,128)}, f32[256,1024]{1,0:T(8,128)}, f32[1024,2,656]{0,2,1:T(8,128)}, f32[656,1024]{1,0:T(8,128)}) async-done(((f32[1024,3,256]{2,0,1:T(8,128)}, f32[256,1024]{1,0:T(8,128)}, f32[1024,2,656]{0,2,1:T(8,128)}, f32[656,1024]{1,0:T(8,128)}), (f32[1024,3,256]{2,0,1:T(8,128)}, f32[256,1024]{1,0:T(8,128)}, f32[1024,2,656]{0,2,1:T(8,128)}, ...) | async-done | bytes 12255248 | tf_op jit(solution)/shard_map/psum | solution.py:269
  669.0 3.9 copy.96
  (225 shorter events, 111.8 us)
Async XLA Ops:
  7.2 180.8 %copy-start = (bf16[1024,2,656]{0,2,1:T(8,128)(2,1)S(1)}, bf16[1024,2,656]{0,2,1:T(8,128)(2,1)}, u32[]{:S(2)}) copy-start(bf16[1024,2,656]{0,2,1:T(8,128)(2,1)} %param.19) | copy-start | bytes 8060932
  7.2 54.0 %all-gather.5.cloned.1.call-start = ((), (), s32[]{:S(2)}) async-start(), calls=%async_computation.5 | async-start | bytes 2621440 | tf_op jit(solution)/shard_map/all_gather | solution.py:171
  8.6 6.8 copy-start.21
  12.7 125.0 %reduce-scatter.8.cloned.1.call-start = ((), (), s32[]{:S(2)}) async-start(), calls=%async_computation.6 | async-start | bytes 2621440 | tf_op jit(solution)/shard_map/reduce_scatter | solution.py:184
  95.1 45.5 %copy-start.31 = (f32[1024]{0:T(1024)S(1)}, f32[1024]{0:T(1024)}, u32[]{:S(2)}) copy-start(f32[1024]{0:T(1024)} %param.16) | copy-start | bytes 12292
  95.1 92.8 %all-gather.7.cloned.1.call-start = ((), (), s32[]{:S(2)}) async-start(), calls=%async_computation.7 | async-start | bytes 2621440 | tf_op jit(solution)/shard_map/all_gather | solution.py:192
  142.9 91.5 %all-gather.9.cloned.1.call-start = ((), (), s32[]{:S(2)}) async-start(), calls=%async_computation.9 | async-start | bytes 2621440 | tf_op jit(solution)/shard_map/all_gather | solution.py:210
  145.0 145.7 %reduce-scatter.12.cloned.1.call-start = ((), (), s32[]{:S(2)}) async-start(), calls=%async_computation.10 | async-start | bytes 2621440 | tf_op jit(solution)/shard_map/reduce_scatter | solution.py:224
  248.1 88.2 %reduce-scatter.10.cloned.1.call-start = ((), (), s32[]{:S(2)}) async-start(), calls=%async_computation.8 | async-start | bytes 2621440 | tf_op jit(solution)/shard_map/reduce_scatter | solution.py:202
  248.1 42.5 %copy-start.2 = (bf16[1,256,1024]{2,1,0:T(8,128)(2,1)S(1)}, bf16[1,256,1024]{2,1,0:T(8,128)(2,1)}, u32[]{:S(2)}) copy-start(bf16[1,256,1024]{2,1,0:T(8,128)(2,1)} %param.13) | copy-start | bytes 1572868
  248.1 42.5 %copy-start.4 = (bf16[256,1024]{1,0:T(8,128)(2,1)S(1)}, bf16[256,1024]{1,0:T(8,128)(2,1)}, u32[]{:S(2)}) copy-start(bf16[256,1024]{1,0:T(8,128)(2,1)} %reduce-scatter.8.cloned.1.call-done) | copy-start | bytes 1572868
  253.1 83.1 %copy-start.19 = (bf16[1,256,1024]{2,1,0:T(8,128)(2,1)S(1)}, bf16[1,256,1024]{2,1,0:T(8,128)(2,1)}, u32[]{:S(2)}) copy-start(bf16[1,256,1024]{2,1,0:T(8,128)(2,1)} %param.21) | copy-start | bytes 1572868
  253.2 131.3 %all-gather.11.cloned.1.call-start = ((), (), s32[]{:S(2)}) async-start(), calls=%async_computation.11 | async-start | bytes 2621440 | tf_op jit(solution)/shard_map/all_gather | solution.py:234
  339.4 133.9 %reduce-scatter.14.cloned.1.call-start = ((), (), s32[]{:S(2)}) async-start(), calls=%async_computation.12 | async-start | bytes 2621440 | tf_op jit(solution)/shard_map/reduce_scatter | solution.py:256
  430.7 66.5 %reduce-scatter.16.cloned.1.call-start = ((), (), s32[]{:S(2)}) async-start(), calls=%async_computation.13 | async-start | bytes 655360
  435.6 4.7 copy-start.27
  435.6 4.7 copy-start.29
  440.3 33.0 %copy-start.30 = (f32[1024]{0:T(1024)S(1)}, f32[1024]{0:T(1024)}, u32[]{:S(2)}) copy-start(f32[1024]{0:T(1024)} %param.15) | copy-start | bytes 12292
  440.3 33.0 %copy-start.33 = (f32[256]{0:T(256)S(1)}, f32[256]{0:T(256)}, u32[]{:S(2)}) copy-start(f32[256]{0:T(256)} %copy-done.32) | copy-start | bytes 3076
  440.3 33.0 %copy-start.35 = (f32[256]{0:T(256)S(1)}, f32[256]{0:T(256)}, u32[]{:S(2)}) copy-start(f32[256]{0:T(256)} %copy-done.34) | copy-start | bytes 3076
  440.3 35.7 %copy-start.7 = (bf16[32,8,2,512]{3,1,2,0:T(8,128)(2,1)S(1)}, bf16[32,8,2,512]{3,1,2,0:T(8,128)(2,1)}, u32[]{:S(2)}) copy-start(bf16[32,8,2,512]{3,1,2,0:T(8,128)(2,1)} %copy-done.6) | copy-start | bytes 1572868
  476.0 193.1 %all-reduce.3.cloned.1.call-start = ((), (), s32[]{:S(2)}) async-start(), calls=%async_computation.14 | async-start | bytes 24510464 | tf_op jit(solution)/shard_map/psum | solution.py:269
  669.0 6.2 copy-start.5
  675.3 5.2 copy-start.1
  (39 other events, 84.0 us)
Sparse Core Ops, SparseCore 0:
  12.8 48.3 all-gather.4
  95.2 42.4 reduce-scatter.7
  143.0 44.8 all-gather.6
  189.9 44.4 all-gather.8
  248.2 42.4 reduce-scatter.11
  293.4 42.8 reduce-scatter.9
  339.5 44.8 all-gather.10
  430.8 42.4 reduce-scatter.13
  476.1 21.0 reduce-scatter.15
  501.7 167.2 all-reduce.2
where the time goes:
time: 696 us; the launch traced here: 688 us
  waiting for transfers between devices  495 us (71%)
  matrix products  83.7 us (12%)
  local copies, waits for them, and re-layouts  42.8 us (6%)
  other arithmetic  35.1 us (5%)
  between operations  15.1 us (2%)
  blocking collectives  12.3 us (2%)
    psum x1, waiting for transfers between devices, shards(): lax.psum((grad_qkv, grad_out_w, grad_in, grad_down, gain_both), 'dp')  158 us
    all_gather x1, waiting for transfers between devices, shards(): gathered_attn = lax.all_gather(normed_attn, 'tensor', axis=0, tiled=True)  44 us
    reduce_scatter x1, waiting for transfers between devices, shards(): lax.psum_scatter(jnp.dot(rows_blk, w_down, preferred_element_type=jnp.flo...  43.9 us
    all_gather x1, waiting for transfers between devices, shards(): gathered_mlp = lax.all_gather(normed_mlp, 'tensor', axis=0, tiled=True)  42.7 us
    reduce_scatter x1, waiting for transfers between devices, shards(): lax.psum_scatter(jnp.dot(rows_blk, w_out, preferred_element_type=jnp.floa...  42.5 us
    all_gather x1, waiting for transfers between devices, shards(): lax.all_gather(d_mid.astype(jnp.bfloat16), 'tensor', axis=0, tiled=True)  41.2 us
    all_gather x1, waiting for transfers between devices, shards(): lax.all_gather(grad_top.astype(jnp.bfloat16), 'tensor', axis=0, tiled=True)  40.2 us
    reduce_scatter x1, waiting for transfers between devices, shards(): lax.psum_scatter(lax.dot_general(rows_blk, w_in, (((1, 2), (1, 2)), ((),...  37.5 us
  transfers between devices with their start and end apart: 10, of which 10 were waited for; matrix products, arithmetic and copies ran while one was open for 6% of the time, Pallas kernels for 0%

commit v1 on v0

--- a/solution.py
+++ b/solution.py
@@ -1,8 +1,11 @@
+import functools
 import math
 
 import jax
 import jax.numpy as jnp
 from jax import lax
+from jax.experimental import pallas as pl
+from jax.experimental.pallas import tpu as pltpu
 from jax.sharding import PartitionSpec as P
 
 HEAD_DIM = 64
@@ -150,6 +153,145 @@
         one_block, (zero_rows, zero_rows), jnp.arange(total_rows // block_rows, dtype=jnp.int32)
     )
     return (query_blocks.reshape(queries.shape), acc_pair[0], acc_pair[1])
+
+
+def bit_orders(n_dp):
+    bits = [1 << i for i in range(n_dp.bit_length() - 1)]
+    rest = bits[1:]
+    turn = len(rest) // 2
+    return (bits, bits[:1] + rest[turn:] + rest[:turn])
+
+
+def grad_reduce_kernel(n_dp, n_arr, *refs):
+    orders = bit_orders(n_dp)
+    n_stage = len(orders[0])
+    x_refs = refs[:n_arr]
+    out_refs = refs[n_arr : 2 * n_arr]
+    pos = 2 * n_arr
+    gath = refs[pos : pos + n_arr]
+    pos += n_arr
+    recv = [refs[pos + s * n_arr : pos + (s + 1) * n_arr] for s in range(n_stage)]
+    pos += n_stage * n_arr
+    work = [refs[pos + s * n_arr : pos + (s + 1) * n_arr] for s in range(n_stage - 1)]
+    pos += (n_stage - 1) * n_arr
+    send_sem, recv_sem = refs[pos], refs[pos + 1]
+    me = lax.axis_index("dp")
+    mine = lax.axis_index("tensor")
+
+    def bit_of(bit):
+        return lax.rem(me // bit, 2)
+
+    def partner_of(bit):
+        return me + bit - 2 * bit * bit_of(bit)
+
+    def remote(src, dst, step, half, arr, bit):
+        return pltpu.make_async_remote_copy(
+            src_ref=src,
+            dst_ref=dst,
+            send_sem=send_sem.at[step, half, arr],
+            recv_sem=recv_sem.at[step, half, arr],
+            device_id=(partner_of(bit), mine),
+            device_id_type=pl.DeviceIdType.MESH,
+        )
+
+    barrier = pltpu.get_barrier_semaphore()
+    for bit in orders[0]:
+        pl.semaphore_signal(
+            barrier, inc=1, device_id=(partner_of(bit), mine), device_id_type=pl.DeviceIdType.MESH
+        )
+    pl.semaphore_wait(barrier, n_stage)
+
+    offs = [[0], [0]]
+    for stage in range(n_stage):
+        size = n_dp >> (stage + 1)
+        copies = []
+        for half in range(2):
+            bit = orders[half][stage]
+            offs[half].append(offs[half][-1] + bit_of(bit) * size)
+            for arr in range(n_arr):
+                src = x_refs[arr] if stage == 0 else work[stage - 1][arr]
+                away = (1 - bit_of(bit)) * size
+                copies.append(
+                    remote(
+                        src.at[half, pl.ds(away, size)],
+                        recv[stage][arr].at[half],
+                        stage,
+                        half,
+                        arr,
+                        bit,
+                    )
+                )
+                copies[-1].start()
+        for half in range(2):
+            kept = bit_of(orders[half][stage]) * size
+            for arr in range(n_arr):
+                copies[half * n_arr + arr].wait_recv()
+                src = x_refs[arr] if stage == 0 else work[stage - 1][arr]
+                last = stage == n_stage - 1
+                base = offs[half][-1] if last else 0
+                dst = gath[arr] if last else work[stage][arr]
+
+                def add_one(i, carry, src=src, dst=dst, kept=kept, base=base, half=half, arr=arr):
+                    total = src[half, kept + i].astype(jnp.float32) + recv[stage][arr][
+                        half, i
+                    ].astype(jnp.float32)
+                    dst[half, base + i] = total.astype(jnp.bfloat16)
+                    return carry
+
+                lax.fori_loop(0, size, add_one, 0)
+        for copy in copies:
+            copy.wait_send()
+    for stage in reversed(range(n_stage)):
+        size = n_dp >> (stage + 1)
+        copies = []
+        for half in range(2):
+            bit = orders[half][stage]
+            start = offs[half][stage + 1]
+            for arr in range(n_arr):
+                part = gath[arr].at[half, pl.ds(start, size)]
+                copies.append(remote(part, part, n_stage + stage, half, arr, bit))
+                copies[-1].start()
+        for copy in copies:
+            copy.wait()
+    for arr in range(n_arr):
+        for half in range(2):
+
+            def move_one(i, carry, arr=arr, half=half):
+                out_refs[arr][half, i] = gath[arr][half, i]
+                return carry
+
+            lax.fori_loop(0, n_dp, move_one, 0)
+
+
+def grad_reduce(grads, call_id):
+    n_dp = lax.axis_size("dp")
+    rows = grads[0].shape[0]
+    if n_dp < 4 or n_dp & (n_dp - 1) or rows % (2 * n_dp):
+        return [lax.psum(g.astype(jnp.bfloat16), "dp") for g in grads]
+    n_arr = len(grads)
+    n_stage = n_dp.bit_length() - 1
+    part = rows // (2 * n_dp)
+    cols = [g.shape[1] for g in grads]
+    args = [g.astype(jnp.bfloat16).reshape(2, n_dp, part, c) for g, c in zip(grads, cols)]
+    scratch = [pltpu.VMEM((2, n_dp, part, c), jnp.bfloat16) for c in cols]
+    for stage in range(n_stage):
+        scratch += [pltpu.VMEM((2, n_dp >> (stage + 1), part, c), jnp.bfloat16) for c in cols]
+    for stage in range(n_stage - 1):
+        scratch += [pltpu.VMEM((2, n_dp >> (stage + 1), part, c), jnp.bfloat16) for c in cols]
+    scratch += [pltpu.SemaphoreType.DMA((2 * n_stage, 2, n_arr))] * 2
+    moved = 2 * sum(rows * c for c in cols)
+    outs = pl.pallas_call(
+        functools.partial(grad_reduce_kernel, n_dp, n_arr),
+        out_shape=[jax.ShapeDtypeStruct(a.shape, jnp.bfloat16) for a in args],
+        in_specs=[pl.BlockSpec(memory_space=pltpu.VMEM)] * n_arr,
+        out_specs=[pl.BlockSpec(memory_space=pltpu.VMEM)] * n_arr,
+        scratch_shapes=scratch,
+        cost_estimate=pl.CostEstimate(flops=0, bytes_accessed=30 * moved, transcendentals=0),
+        compiler_params=pltpu.CompilerParams(
+            collective_id=call_id, has_side_effects=True, vmem_limit_bytes=40 << 20
+        ),
+    )(*args)
+    return [o.reshape(rows, c) for o, c in zip(outs, cols)]
 
 
 def shards(hidden_in, segment_ids, gain_attn, gain_mlp, w_qkv, w_out, w_in, w_down, out_grad):
@@ -169,6 +311,11 @@
     rows_f = hidden_in[0].astype(jnp.float32)
     normed_attn, hat_attn, inv_attn = norm_fwd(rows_f, gain_attn)
     gathered_attn = lax.all_gather(normed_attn, "tensor", axis=0, tiled=True)
+    grad_top = out_grad[0].astype(jnp.float32) * valid_rows[:, None]
+    gathered_attn, grad_top_bf = lax.optimization_barrier(
+        (gathered_attn, grad_top.astype(jnp.bfloat16))
+    )
+    grad_all = lax.all_gather(grad_top_bf, "tensor", axis=0, tiled=True)
     projected = jnp.dot(
         gathered_attn,
         w_qkv.reshape(model_width, 3 * width_local),
@@ -180,9 +327,10 @@
     value_rows = projected[:, 2].astype(jnp.bfloat16)
     att_out, lse_rows = attend_fwd(queries, key_rows, value_rows, seg_row)
     att_flat = att_out.reshape(total_rows, width_local)
-    rows_blk = att_flat
+    att_part = jnp.dot(att_flat, w_out, preferred_element_type=jnp.float32).astype(jnp.bfloat16)
+    att_part, grad_all = lax.optimization_barrier((att_part, grad_all))
     att_sum = lax.psum_scatter(
-        jnp.dot(rows_blk, w_out, preferred_element_type=jnp.float32).astype(jnp.bfloat16),
+        att_part,
         "tensor",
         scatter_dimension=0,
         tiled=True,
@@ -198,43 +346,42 @@
     gate_part = pre_act[:, 1]
     act_up = gelu_val(up_part)
     mixed_act = (act_up * gate_part).astype(jnp.bfloat16)
-    rows_blk = mixed_act
-    mlp_sum = lax.psum_scatter(
-        jnp.dot(rows_blk, w_down, preferred_element_type=jnp.float32).astype(jnp.bfloat16),
-        "tensor",
-        scatter_dimension=0,
-        tiled=True,
-    ).astype(jnp.float32)
-    final_rows = (mid_rows + mlp_sum).astype(jnp.bfloat16)
-    grad_top = out_grad[0].astype(jnp.float32) * valid_rows[:, None]
-    grad_all = lax.all_gather(grad_top.astype(jnp.bfloat16), "tensor", axis=0, tiled=True)
-    grad_down = lax.dot_general(
-        mixed_act, grad_all, (((0,), (0,)), ((), ())), preferred_element_type=jnp.float32
-    )
+    mlp_part = jnp.dot(mixed_act, w_down, preferred_element_type=jnp.float32).astype(jnp.bfloat16)
     d_mixed = lax.dot_general(
         grad_all, w_down, (((1,), (1,)), ((), ())), preferred_element_type=jnp.float32
     )
     d_up = d_mixed * gate_part * gelu_slope(up_part)
     d_gate = d_mixed * act_up
     d_pre = jnp.stack([d_up, d_gate], axis=1).astype(jnp.bfloat16)
+    d_norm_part = lax.dot_general(
+        d_pre, w_in, (((1, 2), (1, 2)), ((), ())), preferred_element_type=jnp.float32
+    ).astype(jnp.bfloat16)
+    d_norm_part, d_pre = lax.optimization_barrier((d_norm_part, d_pre))
+    d_norm_mlp = lax.psum_scatter(d_norm_part, "tensor", scatter_dimension=0, tiled=True)
     grad_in = lax.dot_general(
-        gathered_mlp, d_pre, (((0,), (0,)), ((), ())), preferred_element_type=jnp.float32
-    )
-    rows_blk = d_pre
-    d_norm_mlp = lax.psum_scatter(
-        lax.dot_general(
-            rows_blk, w_in, (((1, 2), (1, 2)), ((), ())), preferred_element_type=jnp.float32
-        ).astype(jnp.bfloat16),
-        "tensor",
-        scatter_dimension=0,
-        tiled=True,
-    ).astype(jnp.float32)
+        gathered_mlp,
+        d_pre.reshape(total_rows, 2 * ff_local),
+        (((0,), (0,)), ((), ())),
+        preferred_element_type=jnp.float32,
+    ).astype(jnp.bfloat16)
+    grad_down = lax.dot_general(
+        grad_all, mixed_act, (((0,), (0,)), ((), ())), preferred_element_type=jnp.float32
+    ).astype(jnp.bfloat16)
+    d_norm_mlp, grad_in, grad_down, mlp_part = lax.optimization_barrier(
+        (d_norm_mlp, grad_in, grad_down, mlp_part)
+    )
+    d_norm_mlp = d_norm_mlp.astype(jnp.float32)
     gain_mlp_part = jnp.sum(d_norm_mlp * hat_mlp, axis=0)
     d_mid = grad_top + norm_bwd(d_norm_mlp, hat_mlp, inv_mlp, gain_mlp)
-    d_mid_all = lax.all_gather(d_mid.astype(jnp.bfloat16), "tensor", axis=0, tiled=True)
-    grad_out_w = lax.dot_general(
-        att_flat, d_mid_all, (((0,), (0,)), ((), ())), preferred_element_type=jnp.float32
-    )
+    d_mid_bf, grad_in, grad_down = lax.optimization_barrier(
+        (d_mid.astype(jnp.bfloat16), grad_in, grad_down)
+    )
+    d_mid_all = lax.all_gather(d_mid_bf, "tensor", axis=0, tiled=True)
+    grad_in, grad_down = grad_reduce([grad_in, grad_down], 0)
+    d_mid_all, grad_in, grad_down, mlp_part = lax.optimization_barrier(
+        (d_mid_all, grad_in, grad_down, mlp_part)
+    )
+    mlp_sum = lax.psum_scatter(mlp_part, "tensor", scatter_dimension=0, tiled=True)
     d_att = lax.dot_general(
         d_mid_all, w_out, (((1,), (1,)), ((), ())), preferred_element_type=jnp.float32
     )
@@ -249,26 +396,36 @@
         .reshape(total_rows, 3, width_local)
         .astype(jnp.bfloat16)
     )
+    d_attn_part = lax.dot_general(
+        d_proj, w_qkv, (((1, 2), (1, 2)), ((), ())), preferred_element_type=jnp.float32
+    ).astype(jnp.bfloat16)
+    d_attn_part, mlp_sum, d_proj = lax.optimization_barrier((d_attn_part, mlp_sum, d_proj))
+    final_rows = (mid_rows + mlp_sum.astype(jnp.float32)).astype(jnp.bfloat16)
+    d_norm_attn = lax.psum_scatter(d_attn_part, "tensor", scatter_dimension=0, tiled=True)
     grad_qkv = lax.dot_general(
-        gathered_attn, d_proj, (((0,), (0,)), ((), ())), preferred_element_type=jnp.float32
-    )
-    rows_blk = d_proj
-    d_norm_attn = lax.psum_scatter(
-        lax.dot_general(
-            rows_blk, w_qkv, (((1, 2), (1, 2)), ((), ())), preferred_element_type=jnp.float32
-        ).astype(jnp.bfloat16),
-        "tensor",
-        scatter_dimension=0,
-        tiled=True,
-    ).astype(jnp.float32)
+        gathered_attn,
+        d_proj.reshape(total_rows, 3 * width_local),
+        (((0,), (0,)), ((), ())),
+        preferred_element_type=jnp.float32,
+    )
+    grad_out_w = lax.dot_general(
+        d_mid_all, att_flat, (((0,), (0,)), ((), ())), preferred_element_type=jnp.float32
+    )
+    grad_qkv, grad_out_w = grad_reduce([grad_qkv, grad_out_w], 1)
+    d_norm_attn, grad_qkv, grad_out_w = lax.optimization_barrier(
+        (d_norm_attn, grad_qkv, grad_out_w)
+    )
+    d_norm_attn = d_norm_attn.astype(jnp.float32)
     gain_attn_part = jnp.sum(d_norm_attn * hat_attn, axis=0)
     d_rows = d_mid + norm_bwd(d_norm_attn, hat_attn, inv_attn, gain_attn)
     gain_both = lax.psum_scatter(
         jnp.stack([gain_attn_part, gain_mlp_part]), "tensor", scatter_dimension=1, tiled=True
     )
-    grad_qkv, grad_out_w, grad_in, grad_down, gain_both = lax.psum(
-        (grad_qkv, grad_out_w, grad_in, grad_down, gain_both), "dp"
-    )
+    gain_both = lax.psum(gain_both, "dp")
+    grad_qkv = grad_qkv.astype(jnp.float32).reshape(model_width, 3, width_local)
+    grad_in = grad_in.astype(jnp.float32).reshape(model_width, 2, ff_local)
+    grad_out_w = jnp.transpose(grad_out_w.astype(jnp.float32))
+    grad_down = jnp.transpose(grad_down.astype(jnp.float32))
     return (
         final_rows[None],
         d_rows[None],

time: 696 us -> 499 us (0.72)
  waiting for transfers between devices: 495 us -> 183 us
  Pallas kernels: 0 us -> 82.8 us
  local copies, waits for them, and re-layouts: 42.8 us -> 58.3 us
  other arithmetic: 35.1 us -> 48.1 us
  loops' own time: 3.18 us -> 11.5 us
    psum x1 -> x0, waiting for transfers between devices: 158 us -> none  [shards(): lax.psum((grad_qkv, grad_out_w, grad_in, grad_down, gain_both), 'dp')]
    pallas_call x0 -> x2, Pallas kernels: none -> 82.8 us  [grad_reduce(): pl.pallas_call(functools.partial(grad_reduce_kernel, n_dp, n_arr), out_sh...]
    reduce_scatter x4, waiting for transfers between devices: 153 us -> 73.4 us  [the longest x1 45.3 us: shards(): lax.psum_scatter(att_part, 'tensor', scatter_dimension=0, tiled=True)]
    all_gather x2, waiting for transfers between devices: 81.4 us -> 11.8 us  [the longest x1 11.8 us: shards(): grad_all = lax.all_gather(grad_top_bf, 'tensor', axis=0, tiled=True)]
    optimization_barrier x0 -> x6, local copies, waits for them, and re-layouts: none -> 14.3 us  [the longest x2 5.87 us: shards(): lax.optimization_barrier((d_mid.astype(jnp.bfloat16), grad_in, grad_down))]
    another operation x1, loops' own time: 1.75 us -> 10.1 us  [attend_bwd(): lax.scan(one_block, (zero_rows, zero_rows), jnp.arange(total_rows // bloc...]
    unnamed x11 -> x10, waiting for transfers between devices: 15.3 us -> 10.1 us
    unnamed x78 -> x95, local copies, waits for them, and re-layouts: 21.5 us -> 16.9 us
  transfers between devices with their start and end apart: 10 -> 9, of which waited for: 10 -> 6; matrix products, arithmetic and copies ran while one was open for 6% -> 27% of each run, Pallas kernels for 0% -> 17%
where the time goes in v1:
time: 499 us; the launch traced here: 493 us
  waiting for transfers between devices  183 us (37%)
  Pallas kernels  82.8 us (17%)
  matrix products  82.4 us (17%)
  local copies, waits for them, and re-layouts  58.3 us (12%)
  other arithmetic  48.1 us (10%)
  between operations  14.7 us (3%)
  blocking collectives  12 us (2%)
  loops' own time  11.5 us (2%)
    pallas_call x2, Pallas kernels, grad_reduce(): pl.pallas_call(functools.partial(grad_reduce_kernel, n_dp, n_arr), out_sh...  82.8 us
    reduce_scatter x1, waiting for transfers between devices, shards(): lax.psum_scatter(att_part, 'tensor', scatter_dimension=0, tiled=True)  45.3 us
    all_gather x1, waiting for transfers between devices, shards(): gathered_mlp = lax.all_gather(normed_mlp, 'tensor', axis=0, tiled=True)  44.7 us
    all_gather x1, waiting for transfers between devices, shards(): gathered_attn = lax.all_gather(normed_attn, 'tensor', axis=0, tiled=True)  42.9 us
    reduce_scatter x1, waiting for transfers between devices, shards(): lax.psum_scatter(d_norm_part, 'tensor', scatter_dimension=0, tiled=True)  28.1 us
    unnamed x95, local copies, waits for them, and re-layouts  16.9 us
    psum x1, blocking collectives, shards(): gain_both = lax.psum(gain_both, 'dp')  12 us
    all_gather x1, waiting for transfers between devices, shards(): grad_all = lax.all_gather(grad_top_bf, 'tensor', axis=0, tiled=True)  11.8 us
  transfers between devices with their start and end apart: 9, of which 6 were waited for; matrix products, arithmetic and copies ran while one was open for 27% of the time, Pallas kernels for 17%

profile of v1, /device:TPU:0, one launch (start us, length us, event | category | flops | bytes accessed | tf_op | source)
XLA Modules:
  0.0 493.3 jit_solution(10361606049876817861)
XLA Ops:
  17.8 42.9 %all-gather.5.cloned.1.call-done = bf16[1024,1024]{1,0:T(8,128)(2,1)} async-done(((bf16[256,1024]{1,0:T(8,128)(2,1)}), bf16[1024,1024]{1,0:T(8,128)(2,1)}) %all-gather.5.cloned.1.call-update) | async-done | bytes 2097168 | tf_op jit(solution)/shard_map/all_gather | solution.py:313
  60.7 3.9 fusion.44
  72.9 22.3 %while.27 = (s32[]{:T(128)}, bf16[2,512,4,64]{1,3,2,0:T(8,128)(2,1)}, f32[2,4,512]{2,1,0:T(4,128)S(1)}, s32[2]{0:T(128)S(1)}, s32[1024]{0:T(1024)S(1)}, /*index=...) while((s32[]{:T(128)}, ...), condition=%wide.region_6.7_spmd, body=%wide.region_3.6_spmd.sunk | while | flops 562690048 | bytes 33106184 | solution.py:101
  79.6 3.7 fusion.136
  90.7 3.7 fusion.136
  100.7 11.8 %all-gather.7.cloned.1.call-done = bf16[1024,1024]{1,0:T(8,128)(2,1)} async-done(((bf16[256,1024]{1,0:T(8,128)(2,1)}), bf16[1024,1024]{1,0:T(8,128)(2,1)}) %all-gather.7.cloned.1.call-update) | async-done | bytes 2097168 | tf_op jit(solution)/shard_map/all_gather | solution.py:318
  112.6 45.3 %reduce-scatter.8.cloned.1.call-done = bf16[256,1024]{1,0:T(8,128)(2,1)} async-done(((bf16[1024,1024]{1,0:T(8,128)(2,1)}), bf16[256,1024]{1,0:T(8,128)(2,1)}) %reduce-scatter.8.cloned.1.call-update) | async-done | bytes 524304 | tf_op jit(solution)/shard_map/reduce_scatter | solution.py:332
  163.4 44.7 %all-gather.9.cloned.1.call-done = bf16[1024,1024]{1,0:T(8,128)(2,1)} async-done(((bf16[256,1024]{1,0:T(8,128)(2,1)}), bf16[1024,1024]{1,0:T(8,128)(2,1)}) %all-gather.9.cloned.1.call-update) | async-done | bytes 2097168 | tf_op jit(solution)/shard_map/all_gather | solution.py:340
  208.1 4.7 fusion.42
  212.8 3.8 fusion.48
  218.2 4.6 bitcast_convert_fusion.1
  222.8 3.6 pad_maximum_fusion
  226.6 4.1 convolution_convert_fusion.4
  233.9 7.0 %convolution_convert_fusion = bf16[1024,1312]{0,1:T(8,128)(2,1)} fusion(bf16[1024,1312]{0,1:T(8,128)(2,1)} %bitcast.278, bf16[1024,1024]{1,0:T(8,128)(2,1)} %all-gather.9.cloned.1.call-done), kind=kOutput, calls=%fused_computation.47 | convolution fusion | flops 2752806912 | bytes 7471104 | tf_op jit(solution)/shard_map/dot_general | solution.py:361
  240.9 28.1 %reduce-scatter.10.cloned.1.call-done = bf16[256,1024]{1,0:T(8,128)(2,1)} async-done(((bf16[1024,1024]{1,0:T(8,128)(2,1)}), bf16[256,1024]{1,0:T(8,128)(2,1)}) %reduce-scatter.10.cloned.1.call-update) | async-done | bytes 524304 | tf_op jit(solution)/shard_map/reduce_scatter | solution.py:360
  283.5 53.0 %shard_map.152 = (bf16[2,8,64,1312]{3,2,1,0:T(8,128)(2,1)S(1)}, bf16[2,8,64,656]{3,2,1,0:T(8,128)(2,1)S(1)}) custom-call(bf16[2,8,64,1312]{3,2,1,0:T(8,128)(2,1)S(1)} %bitcast.264, bf16[2,8,64,656]{3,2,1,0:T(8,128)(2,1)S(1)} %bitcast.265), custom_call_target="tpu_custom_call" | custom-call | bytes 120913920 | tf_op jit(solution)/shard_map/pallas_call | solution.py:283
  339.3 3.7 multiply_reduce_fusion
  343.0 36.8 %while.28 = (s32[]{:T(128)}, f32[1024,4,64]{0,2,1:T(8,128)S(1)}, f32[1024,4,64]{0,2,1:T(8,128)}, f32[2,512,4,64]{1,3,2,0:T(8,128)}, s32[2]{0:T(128)S(1)}, /*inde...) while((s32[]{:T(128)}, f32[1024,4,64]{0,2,1:T(8,128)S(1)}, ...), condition=%wide.region_15.16_spmd.clone, body=%wide.region_14.15_spmd.clone.sunk | while | flops 1365114880 | bytes 65603988 | solution.py:152
  357.3 4.7 multiply_convert_fusion.5
  371.4 4.8 multiply_convert_fusion.5
  414.8 3.9 convolution_convert_fusion.3
  418.7 29.9 %shard_map.153 = (bf16[2,8,64,768]{3,2,1,0:T(8,128)(2,1)S(1)}, bf16[2,8,64,256]{3,2,1,0:T(8,128)(2,1)S(1)}) custom-call(bf16[2,8,64,768]{3,2,1,0:T(8,128)(2,1)S(1)} %bitcast.269, bf16[2,8,64,256]{3,2,1,0:T(8,128)(2,1)S(1)} %bitcast.271), custom_call_target="tpu_custom_call" | custom-call | bytes 62914560 | tf_op jit(solution)/shard_map/pallas_call | solution.py:283
  463.1 9.9 %reduce-scatter.16.cloned.1.call-done = f32[256,2]{1,0:T(8,128)} async-done(((f32[1024,2]{1,0:T(8,128)}), f32[256,2]{1,0:T(8,128)}) %reduce-scatter.16.cloned.1.call-update) | async-done | bytes 2064
  474.0 12.0 %psum.7 = f32[2,256]{1,0:T(2,128)S(1)} all-reduce(f32[2,256]{1,0:T(2,128)S(1)} %copy.86), channel_id=1, replica_groups=mesh['dp'=8,'tensor'=4] {'dp'}, use_global_device_ids=true, to_apply=%region_23.24 | all-reduce | flops 512 | bytes 4096 | tf_op jit(solution)/shard_map/psum | solution.py:424
  (244 shorter events, 133.4 us)
Async XLA Ops:
  7.2 200.9 %copy-start = (bf16[1024,2,656]{0,2,1:T(8,128)(2,1)S(1)}, bf16[1024,2,656]{0,2,1:T(8,128)(2,1)}, u32[]{:S(2)}) copy-start(bf16[1024,2,656]{0,2,1:T(8,128)(2,1)} %param.19) | copy-start | bytes 8060932
  7.2 53.5 %all-gather.5.cloned.1.call-start = ((), (), s32[]{:S(2)}) async-start(), calls=%async_computation.5 | async-start | bytes 2621440 | tf_op jit(solution)/shard_map/all_gather | solution.py:313
  8.6 6.8 %copy-start.42 = (f32[256]{0:T(256)}, f32[256]{0:T(256)S(1)}, u32[]{:S(2)}) copy-start(f32[256]{0:T(256)S(1)} %broadcast_multiply_fusion.7) | copy-start | bytes 3076
  9.9 6.9 %copy-start.28 = (bf16[1,256,1024]{2,1,0:T(8,128)(2,1)S(1)}, bf16[1,256,1024]{2,1,0:T(8,128)(2,1)}, u32[]{:S(2)}) copy-start(bf16[1,256,1024]{2,1,0:T(8,128)(2,1)} %param.21) | copy-start | bytes 1572868
  12.2 100.3 %all-gather.7.cloned.1.call-start = ((), (), s32[]{:S(2)}) async-start(), calls=%async_computation.6 | async-start | bytes 2621440 | tf_op jit(solution)/shard_map/all_gather | solution.py:318
  67.9 90.0 %reduce-scatter.8.cloned.1.call-start = ((), (), s32[]{:S(2)}) async-start(), calls=%async_computation.7 | async-start | bytes 2621440 | tf_op jit(solution)/shard_map/reduce_scatter | solution.py:332
  100.7 60.0 %copy-start.41 = (f32[1024]{0:T(1024)S(1)}, f32[1024]{0:T(1024)}, u32[]{:S(2)}) copy-start(f32[1024]{0:T(1024)} %param.16) | copy-start | bytes 12292
  112.5 95.5 %all-gather.9.cloned.1.call-start = ((), (), s32[]{:S(2)}) async-start(), calls=%async_computation.8 | async-start | bytes 2621440 | tf_op jit(solution)/shard_map/all_gather | solution.py:340
  163.0 106.0 %reduce-scatter.10.cloned.1.call-start = ((), (), s32[]{:S(2)}) async-start(), calls=%async_computation.9 | async-start | bytes 2621440 | tf_op jit(solution)/shard_map/reduce_scatter | solution.py:360
  226.5 112.8 %all-gather.11.cloned.1.call-start = ((), (), s32[]{:S(2)}) async-start(), calls=%async_computation.10 | async-start | bytes 2621440 | tf_op jit(solution)/shard_map/all_gather | solution.py:379
  233.9 35.1 %copy-start.8 = (bf16[1,256,1024]{2,1,0:T(8,128)(2,1)S(1)}, bf16[1,256,1024]{2,1,0:T(8,128)(2,1)}, u32[]{:S(2)}) copy-start(bf16[1,256,1024]{2,1,0:T(8,128)(2,1)} %param.13) | copy-start | bytes 1572868
  233.9 35.1 %copy-start.11 = (bf16[256,1024]{1,0:T(8,128)(2,1)S(1)}, bf16[256,1024]{1,0:T(8,128)(2,1)}, u32[]{:S(2)}) copy-start(bf16[256,1024]{1,0:T(8,128)(2,1)} %reduce-scatter.8.cloned.1.call-done) | copy-start | bytes 1572868
  233.9 36.8 %copy-start.29 = (bf16[1,256,1024]{2,1,0:T(8,128)(2,1)S(1)}, bf16[1,256,1024]{2,1,0:T(8,128)(2,1)}, u32[]{:S(2)}) copy-start(bf16[1,256,1024]{2,1,0:T(8,128)(2,1)} %param.21) | copy-start | bytes 1572868
  240.9 32.7 %copy-start.19 = (f32[1024,64]{0,1:T(8,128)S(1)}, f32[1024,64]{0,1:T(8,128)}, u32[]{:S(2)}) copy-start(f32[1024,64]{0,1:T(8,128)} %get-tuple-element.331) | copy-start | bytes 786436
  273.5 128.9 %reduce-scatter.12.cloned.1.call-start = ((), (), s32[]{:S(2)}) async-start(), calls=%async_computation.11 | async-start | bytes 2621440 | tf_op jit(solution)/shard_map/reduce_scatter | solution.py:384
  339.3 110.5 %reduce-scatter.14.cloned.1.call-start = ((), (), s32[]{:S(2)}) async-start(), calls=%async_computation.12 | async-start | bytes 2621440 | tf_op jit(solution)/shard_map/reduce_scatter | solution.py:404
  402.5 70.6 %reduce-scatter.16.cloned.1.call-start = ((), (), s32[]{:S(2)}) async-start(), calls=%async_computation.13 | async-start | bytes 655360
  414.7 35.0 %copy-start.9 = (bf16[1,256,1024]{2,1,0:T(8,128)(2,1)S(1)}, bf16[1,256,1024]{2,1,0:T(8,128)(2,1)}, u32[]{:S(2)}) copy-start(bf16[1,256,1024]{2,1,0:T(8,128)(2,1)} %param.13) | copy-start | bytes 1572868
  414.7 35.0 %copy-start.40 = (f32[1024]{0:T(1024)S(1)}, f32[1024]{0:T(1024)}, u32[]{:S(2)}) copy-start(f32[1024]{0:T(1024)} %param.15) | copy-start | bytes 12292
  414.8 35.0 %copy-start.43 = (f32[256]{0:T(256)S(1)}, f32[256]{0:T(256)}, u32[]{:S(2)}) copy-start(f32[256]{0:T(256)} %copy-done.42) | copy-start | bytes 3076
  414.8 35.0 %copy-start.45 = (f32[256]{0:T(256)S(1)}, f32[256]{0:T(256)}, u32[]{:S(2)}) copy-start(f32[256]{0:T(256)} %copy-done.44) | copy-start | bytes 3076
  418.7 34.8 %copy-start.12 = (bf16[256,1024]{1,0:T(8,128)(2,1)S(1)}, bf16[256,1024]{1,0:T(8,128)(2,1)}, u32[]{:S(2)}) copy-start(bf16[256,1024]{1,0:T(8,128)(2,1)} %reduce-scatter.8.cloned.1.call-done) | copy-start | bytes 1572868
  418.7 34.8 %copy-start.21 = (f32[256,1024]{1,0:T(8,128)S(1)}, f32[256,1024]{1,0:T(8,128)}, u32[]{:S(2)}) copy-start(f32[256,1024]{1,0:T(8,128)} %get-tuple-element.301) | copy-start | bytes 3145732
  457.3 29.3 %copy-start.1 = (bf16[1024,2,656]{0,2,1:T(8,128)(2,1)S(1)}, bf16[1024,2,656]{0,2,1:T(8,128)(2,1)}, u32[]{:S(2)}) copy-start(bf16[1024,2,656]{0,2,1:T(8,128)(2,1)} %param.19) | copy-start | bytes 8060932
  (44 other events, 113.4 us)
Sparse Core Ops, SparseCore 0:
  12.3 48.3 all-gather.4
  68.0 44.4 all-gather.6
  115.4 42.4 reduce-scatter.7
  163.2 44.8 all-gather.8
  226.6 42.4 reduce-scatter.9
  273.7 44.8 all-gather.10
  339.4 41.9 reduce-scatter.11
  402.6 41.9 reduce-scatter.13
  452.6 20.3 reduce-scatter.15

commit v2 on v1

--- a/solution.py
+++ b/solution.py
@@ -294,6 +294,86 @@
     return [o.reshape(rows, c) for o, c in zip(outs, cols)]
 
 
+def gain_reduce_kernel(n_dp, n_tp, x_ref, out_ref, stage_buf, from_tp, from_dp, t_send, t_recv, d_send, d_recv, c_sem):
+    me = lax.axis_index("dp")
+    mine = lax.axis_index("tensor")
+    mesh_type = pl.DeviceIdType.MESH
+    barrier = pltpu.get_barrier_semaphore()
+    for k in range(1, n_tp):
+        pl.semaphore_signal(
+            barrier, inc=1, device_id=(me, lax.rem(mine + k, n_tp)), device_id_type=mesh_type
+        )
+    for k in range(1, n_dp):
+        pl.semaphore_signal(
+            barrier, inc=1, device_id=(lax.rem(me + k, n_dp), mine), device_id_type=mesh_type
+        )
+    pl.semaphore_wait(barrier, n_tp + n_dp - 2)
+    copies = []
+    for k in range(1, n_tp):
+        target = lax.rem(mine + k, n_tp)
+        copies.append(
+            pltpu.make_async_remote_copy(
+                src_ref=x_ref.at[target],
+                dst_ref=from_tp.at[k],
+                send_sem=t_send.at[k],
+                recv_sem=t_recv.at[k],
+                device_id=(me, target),
+                device_id_type=mesh_type,
+            )
+        )
+        copies[-1].start()
+    total = x_ref[mine]
+    for k in range(1, n_tp):
+        copies[k - 1].wait()
+        total = total + from_tp[k]
+    stage_buf[...] = total
+    local = pltpu.make_async_copy(stage_buf, from_dp.at[0], c_sem)
+    local.start()
+    local.wait()
+    copies = []
+    for k in range(1, n_dp):
+        copies.append(
+            pltpu.make_async_remote_copy(
+                src_ref=from_dp.at[0],
+                dst_ref=from_dp.at[k],
+                send_sem=d_send.at[k],
+                recv_sem=d_recv.at[k],
+                device_id=(lax.rem(me + k, n_dp), mine),
+                device_id_type=mesh_type,
+            )
+        )
+        copies[-1].start()
+    for k in range(1, n_dp):
+        copies[k - 1].wait()
+        total = total + from_dp[k]
+    out_ref[...] = total
+
+
+def gain_reduce(parts, call_id):
+    n_dp = lax.axis_size("dp")
+    n_tp = lax.axis_size("tensor")
+    wide = parts.shape[1] // n_tp
+    arg = jnp.transpose(parts.reshape(2, n_tp, wide), (1, 0, 2))
+    return pl.pallas_call(
+        functools.partial(gain_reduce_kernel, n_dp, n_tp),
+        out_shape=jax.ShapeDtypeStruct((2, wide), jnp.float32),
+        in_specs=[pl.BlockSpec(memory_space=pltpu.VMEM)],
+        out_specs=pl.BlockSpec(memory_space=pltpu.VMEM),
+        scratch_shapes=[
+            pltpu.VMEM((2, wide), jnp.float32),
+            pltpu.VMEM((n_tp, 2, wide), jnp.float32),
+            pltpu.VMEM((n_dp, 2, wide), jnp.float32),
+            pltpu.SemaphoreType.DMA((n_tp,)),
+            pltpu.SemaphoreType.DMA((n_tp,)),
+            pltpu.SemaphoreType.DMA((n_dp,)),
+            pltpu.SemaphoreType.DMA((n_dp,)),
+            pltpu.SemaphoreType.DMA,
+        ],
+        cost_estimate=pl.CostEstimate(flops=0, bytes_accessed=20 << 20, transcendentals=0),
+        compiler_params=pltpu.CompilerParams(collective_id=call_id, has_side_effects=True),
+    )(arg)
+
+
 def shards(hidden_in, segment_ids, gain_attn, gain_mlp, w_qkv, w_out, w_in, w_down, out_grad):
     n_parts = lax.axis_size("tensor")
     shard_rows = hidden_in.shape[1]
@@ -310,12 +390,10 @@
     valid_rows = (my_seg < total_rows).astype(jnp.float32)
     rows_f = hidden_in[0].astype(jnp.float32)
     normed_attn, hat_attn, inv_attn = norm_fwd(rows_f, gain_attn)
+    normed_attn, out_grad = lax.optimization_barrier((normed_attn, out_grad))
     gathered_attn = lax.all_gather(normed_attn, "tensor", axis=0, tiled=True)
     grad_top = out_grad[0].astype(jnp.float32) * valid_rows[:, None]
-    gathered_attn, grad_top_bf = lax.optimization_barrier(
-        (gathered_attn, grad_top.astype(jnp.bfloat16))
-    )
-    grad_all = lax.all_gather(grad_top_bf, "tensor", axis=0, tiled=True)
+    grad_all = lax.all_gather(grad_top.astype(jnp.bfloat16), "tensor", axis=0, tiled=True)
     projected = jnp.dot(
         gathered_attn,
         w_qkv.reshape(model_width, 3 * width_local),
@@ -358,30 +436,30 @@
     ).astype(jnp.bfloat16)
     d_norm_part, d_pre = lax.optimization_barrier((d_norm_part, d_pre))
     d_norm_mlp = lax.psum_scatter(d_norm_part, "tensor", scatter_dimension=0, tiled=True)
+    grad_down = lax.dot_general(
+        grad_all, mixed_act, (((0,), (0,)), ((), ())), preferred_element_type=jnp.float32
+    ).astype(jnp.bfloat16)
+    (grad_down,) = grad_reduce([grad_down], 2)
     grad_in = lax.dot_general(
         gathered_mlp,
         d_pre.reshape(total_rows, 2 * ff_local),
         (((0,), (0,)), ((), ())),
         preferred_element_type=jnp.float32,
     ).astype(jnp.bfloat16)
-    grad_down = lax.dot_general(
-        grad_all, mixed_act, (((0,), (0,)), ((), ())), preferred_element_type=jnp.float32
-    ).astype(jnp.bfloat16)
     d_norm_mlp, grad_in, grad_down, mlp_part = lax.optimization_barrier(
         (d_norm_mlp, grad_in, grad_down, mlp_part)
     )
     d_norm_mlp = d_norm_mlp.astype(jnp.float32)
     gain_mlp_part = jnp.sum(d_norm_mlp * hat_mlp, axis=0)
     d_mid = grad_top + norm_bwd(d_norm_mlp, hat_mlp, inv_mlp, gain_mlp)
-    d_mid_bf, grad_in, grad_down = lax.optimization_barrier(
-        (d_mid.astype(jnp.bfloat16), grad_in, grad_down)
+    d_mid_bf, grad_in, mlp_part = lax.optimization_barrier(
+        (d_mid.astype(jnp.bfloat16), grad_in, mlp_part)
     )
     d_mid_all = lax.all_gather(d_mid_bf, "tensor", axis=0, tiled=True)
-    grad_in, grad_down = grad_reduce([grad_in, grad_down], 0)
-    d_mid_all, grad_in, grad_down, mlp_part = lax.optimization_barrier(
-        (d_mid_all, grad_in, grad_down, mlp_part)
-    )
     mlp_sum = lax.psum_scatter(mlp_part, "tensor", scatter_dimension=0, tiled=True)
+    (grad_in,) = grad_reduce([grad_in], 0)
+    grad_down = jnp.transpose(grad_down.astype(jnp.float32))
+    d_mid_all, grad_in, grad_down = lax.optimization_barrier((d_mid_all, grad_in, grad_down))
     d_att = lax.dot_general(
         d_mid_all, w_out, (((1,), (1,)), ((), ())), preferred_element_type=jnp.float32
     )
@@ -411,21 +489,20 @@
     grad_out_w = lax.dot_general(
         d_mid_all, att_flat, (((0,), (0,)), ((), ())), preferred_element_type=jnp.float32
     )
+    gain_attn_part = (
+        jnp.sum(d_attn_part.astype(jnp.float32) * gathered_attn.astype(jnp.float32), axis=0)
+        / gain_attn
+    )
+    gain_both = gain_reduce(jnp.stack([gain_attn_part, gain_mlp_part]), 3)
     grad_qkv, grad_out_w = grad_reduce([grad_qkv, grad_out_w], 1)
-    d_norm_attn, grad_qkv, grad_out_w = lax.optimization_barrier(
-        (d_norm_attn, grad_qkv, grad_out_w)
-    )
-    d_norm_attn = d_norm_attn.astype(jnp.float32)
-    gain_attn_part = jnp.sum(d_norm_attn * hat_attn, axis=0)
-    d_rows = d_mid + norm_bwd(d_norm_attn, hat_attn, inv_attn, gain_attn)
-    gain_both = lax.psum_scatter(
-        jnp.stack([gain_attn_part, gain_mlp_part]), "tensor", scatter_dimension=1, tiled=True
-    )
-    gain_both = lax.psum(gain_both, "dp")
     grad_qkv = grad_qkv.astype(jnp.float32).reshape(model_width, 3, width_local)
     grad_in = grad_in.astype(jnp.float32).reshape(model_width, 2, ff_local)
     grad_out_w = jnp.transpose(grad_out_w.astype(jnp.float32))
-    grad_down = jnp.transpose(grad_down.astype(jnp.float32))
+    d_norm_attn, gain_both, grad_qkv, grad_out_w, grad_in = lax.optimization_barrier(
+        (d_norm_attn, gain_both, grad_qkv, grad_out_w, grad_in)
+    )
+    d_norm_attn = d_norm_attn.astype(jnp.float32)
+    d_rows = d_mid + norm_bwd(d_norm_attn, hat_attn, inv_attn, gain_attn)
     return (
         final_rows[None],
         d_rows[None],

time: 499 us -> 464 us (0.930)
  waiting for transfers between devices: 183 us -> 148 us
  Pallas kernels: 82.8 us -> 103 us
  blocking collectives: 12 us -> 0 us
    reduce_scatter x1, waiting for transfers between devices: 28.1 us -> 3.22 us  [shards(): lax.psum_scatter(d_norm_part, 'tensor', scatter_dimension=0, tiled=True)]
    psum x1 -> x0, blocking collectives: 12 us -> none  [shards(): gain_both = lax.psum(gain_both, 'dp')]
    pallas_call x2 -> x3, Pallas kernels: 82.8 us -> 93.2 us  [grad_reduce(): pl.pallas_call(functools.partial(grad_reduce_kernel, n_dp, n_arr), out_sh...]
    pallas_call x0 -> x1, Pallas kernels: none -> 10.2 us  [gain_reduce(): pl.pallas_call(functools.partial(gain_reduce_kernel, n_dp, n_tp), out_sha...]
    unnamed x10 -> x8, waiting for transfers between devices: 10.1 us -> 0.13 us
    optimization_barrier x5 -> x2, local copies, waits for them, and re-layouts: 12.6 us -> 6.01 us  [the longest x1 4.54 us: shards(): lax.optimization_barrier((d_mid.astype(jnp.bfloat16), grad_in, mlp_part))]
    unnamed x95 -> x93, local copies, waits for them, and re-layouts: 16.9 us -> 13 us
  transfers between devices with their start and end apart: 9 -> 8, of which waited for: 6 -> 5; matrix products, arithmetic and copies ran while one was open for 27% -> 29% of each run, Pallas kernels for 17% -> 23%
where the time goes in v2:
time: 464 us; the launch traced here: 459 us
  waiting for transfers between devices  148 us (32%)
  Pallas kernels  103 us (22%)
  matrix products  79.5 us (17%)
  local copies, waits for them, and re-layouts  55.1 us (12%)
  other arithmetic  45.5 us (10%)
  between operations  15 us (3%)
  loops' own time  11.7 us (3%)
    pallas_call x3, Pallas kernels, grad_reduce(): pl.pallas_call(functools.partial(grad_reduce_kernel, n_dp, n_arr), out_sh...  93.2 us
    reduce_scatter x1, waiting for transfers between devices, shards(): lax.psum_scatter(att_part, 'tensor', scatter_dimension=0, tiled=True)  45.3 us
    all_gather x1, waiting for transfers between devices, shards(): gathered_mlp = lax.all_gather(normed_mlp, 'tensor', axis=0, tiled=True)  44.7 us
    all_gather x1, waiting for transfers between devices, shards(): gathered_attn = lax.all_gather(normed_attn, 'tensor', axis=0, tiled=True)  42.2 us
    unnamed x93, local copies, waits for them, and re-layouts  13 us
    all_gather x1, waiting for transfers between devices, shards(): lax.all_gather(grad_top.astype(jnp.bfloat16), 'tensor', axis=0, tiled=True)  12.5 us
    another operation x1, loops' own time, attend_bwd(): lax.scan(one_block, (zero_rows, zero_rows), jnp.arange(total_rows // bloc...  10.2 us
    pallas_call x1, Pallas kernels, gain_reduce(): pl.pallas_call(functools.partial(gain_reduce_kernel, n_dp, n_tp), out_sha...  10.2 us
  transfers between devices with their start and end apart: 8, of which 5 were waited for; matrix products, arithmetic and copies ran while one was open for 29% of the time, Pallas kernels for 23%

profile of v2, /device:TPU:0, one launch (start us, length us, event | category | flops | bytes accessed | tf_op | source)
XLA Modules:
  0.0 458.9 jit_solution(15776382446143779516)
XLA Ops:
  18.4 42.2 %all-gather.5.cloned.1.call-done = bf16[1024,1024]{1,0:T(8,128)(2,1)} async-done(((bf16[256,1024]{1,0:T(8,128)(2,1)}), bf16[1024,1024]{1,0:T(8,128)(2,1)}) %all-gather.5.cloned.1.call-update) | async-done | bytes 2097168 | tf_op jit(solution)/shard_map/all_gather | solution.py:394
  60.7 3.9 fusion.44
  67.9 21.1 %while.27 = (s32[]{:T(128)}, bf16[2,512,4,64]{1,3,2,0:T(8,128)(2,1)}, f32[2,4,512]{2,1,0:T(4,128)S(1)}, s32[2]{0:T(128)S(1)}, s32[1024]{0:T(1024)S(1)}, /*index=...) while((s32[]{:T(128)}, ...), condition=%wide.region_6.7_spmd, body=%wide.region_3.6_spmd.sunk | while | flops 562690048 | bytes 35203364 | solution.py:101
  94.8 12.5 %all-gather.7.cloned.1.call-done = bf16[1024,1024]{1,0:T(8,128)(2,1)} async-done(((bf16[256,1024]{1,0:T(8,128)(2,1)}), bf16[1024,1024]{1,0:T(8,128)(2,1)}) %all-gather.7.cloned.1.call-update) | async-done | bytes 2097168 | tf_op jit(solution)/shard_map/all_gather | solution.py:396
  107.4 45.3 %reduce-scatter.5.cloned.1.call-done = bf16[256,1024]{1,0:T(8,128)(2,1)} async-done(((bf16[1024,1024]{1,0:T(8,128)(2,1)}), bf16[256,1024]{1,0:T(8,128)(2,1)}) %reduce-scatter.5.cloned.1.call-update) | async-done | bytes 524304 | tf_op jit(solution)/shard_map/reduce_scatter | solution.py:410
  158.1 44.7 %all-gather.9.cloned.1.call-done = bf16[1024,1024]{1,0:T(8,128)(2,1)} async-done(((bf16[256,1024]{1,0:T(8,128)(2,1)}), bf16[1024,1024]{1,0:T(8,128)(2,1)}) %all-gather.9.cloned.1.call-update) | async-done | bytes 2097168 | tf_op jit(solution)/shard_map/all_gather | solution.py:418
  202.8 4.7 %fusion.42 = f32[1024,2,656]{0,2,1:T(8,128)S(1)} fusion(bf16[1024,2,656]{0,2,1:T(8,128)(2,1)S(1)} %copy-done, bf16[1024,1024]{1,0:T(8,128)(2,1)} %all-gather.9.cloned.1.call-done), kind=kOutput, calls=%fused_computation.58 | convolution fusion | flops 2751463424 | bytes 10158080 | tf_op jit(solution)/shard_map/dot_general | solution.py:419
  207.6 3.8 fusion.48
  212.9 4.6 %bitcast_convert_fusion.1 = bf16[1024,1024]{1,0:T(8,128)(2,1)} fusion(bf16[1024,2,656]{0,2,1:T(8,128)(2,1)S(1)} %copy-done, bf16[1024,1,656]{0,2,1:T(8,128)(2,1)S(1)} %get-tuple-element.302, bf16[1024,1,656]{0,2,1:T(8,128)(2,1)S(1)} %get-tuple-element.301), kind=kOutput, calls=%fused_computation.44 | convolution fusion | flops 2753855488 | bytes 7471104 | tf_op jit(solution)/shard_map/dot_general | solution.py:434
  217.5 3.6 pad_maximum_fusion
  225.1 25.2 %shard_map.152 = bf16[2,8,64,656]{3,2,1,0:T(8,128)(2,1)S(1)} custom-call(bf16[2,8,64,656]{3,2,1,0:T(8,128)(2,1)S(1)} %bitcast.263), custom_call_target="tpu_custom_call" | custom-call | bytes 40304640 | tf_op jit(solution)/shard_map/pallas_call | solution.py:283
  253.5 7.0 %convolution_convert_fusion = bf16[1024,1312]{0,1:T(8,128)(2,1)} fusion(bf16[1024,1312]{0,1:T(8,128)(2,1)} %bitcast.271, bf16[1024,1024]{1,0:T(8,128)(2,1)} %all-gather.9.cloned.1.call-done), kind=kOutput, calls=%fused_computation.48 | convolution fusion | flops 2752806912 | bytes 7471104 | tf_op jit(solution)/shard_map/dot_general | solution.py:443
  272.3 4.5 copy.50
  278.7 38.0 %shard_map.153 = bf16[2,8,64,1312]{3,2,1,0:T(8,128)(2,1)S(1)} custom-call(bf16[2,8,64,1312]{3,2,1,0:T(8,128)(2,1)S(1)} %bitcast.261), custom_call_target="tpu_custom_call" | custom-call | bytes 80609280 | tf_op jit(solution)/shard_map/pallas_call | solution.py:283
  318.6 3.6 multiply_reduce_fusion.1
  322.3 36.0 %while.28 = (s32[]{:T(128)}, f32[1024,4,64]{0,2,1:T(8,128)}, f32[1024,4,64]{0,2,1:T(8,128)}, f32[2,512,4,64]{1,3,2,0:T(8,128)}, s32[2]{0:T(128)S(1)}, /*index=5*...) while((s32[]{:T(128)}, f32[1024,4,64]{0,2,1:T(8,128)}, ...), condition=%wide.region_15.16_spmd.clone, body=%wide.region_14.15_spmd.clone.sunk | while | flops 1365114880 | bytes 78187016 | solution.py:152
  337.6 3.3 multiply_convert_fusion.5
  351.3 3.3 multiply_convert_fusion.5
  384.5 3.5 copy.62
  392.9 10.2 %shard_map.154 = f32[2,256]{1,0:T(2,128)} custom-call(f32[4,2,256]{2,1,0:T(2,128)} %maximum_bitcast_fusion.x_ref), custom_call_target="tpu_custom_call" | custom-call | bytes 20971520 | tf_op jit(solution)/shard_map/pallas_call | solution.py:357
  404.8 3.9 convolution_convert_fusion.3
  408.7 30.0 %shard_map.155 = (bf16[2,8,64,768]{3,2,1,0:T(8,128)(2,1)S(1)}, bf16[2,8,64,256]{3,2,1,0:T(8,128)(2,1)S(1)}) custom-call(bf16[2,8,64,768]{3,2,1,0:T(8,128)(2,1)S(1)} %bitcast.264, bf16[2,8,64,256]{3,2,1,0:T(8,128)(2,1)S(1)} %bitcast.265), custom_call_target="tpu_custom_call" | custom-call | bytes 62914560 | tf_op jit(solution)/shard_map/pallas_call | solution.py:283
  440.2 3.3 reshape.299
  445.5 4.6 %copy.63 = f32[1024,3,256]{2,0,1:T(8,128)} copy(f32[1024,3,256]{2,1,0:T(4,128)} %reshape.299) | data formatting | bytes 6291456
  (262 shorter events, 126.4 us)
Async XLA Ops:
  7.2 195.7 %copy-start = (bf16[1024,2,656]{0,2,1:T(8,128)(2,1)S(1)}, bf16[1024,2,656]{0,2,1:T(8,128)(2,1)}, u32[]{:S(2)}) copy-start(bf16[1024,2,656]{0,2,1:T(8,128)(2,1)} %param.19) | copy-start | bytes 8060932
  7.2 5.7 %copy-start.29 = (bf16[1,256,1024]{2,1,0:T(8,128)(2,1)S(1)}, bf16[1,256,1024]{2,1,0:T(8,128)(2,1)}, u32[]{:S(2)}) copy-start(bf16[1,256,1024]{2,1,0:T(8,128)(2,1)} %param.21) | copy-start | bytes 1572868
  7.2 6.7 %copy-start.38 = (s32[1,1024]{1,0:T(1,128)S(1)}, s32[1,1024]{1,0:T(1,128)}, u32[]{:S(2)}) copy-start(s32[1,1024]{1,0:T(1,128)} %param.14) | copy-start | bytes 12292
  7.2 53.4 %all-gather.5.cloned.1.call-start = ((), (), s32[]{:S(2)}) async-start(), calls=%async_computation.4 | async-start | bytes 2621440 | tf_op jit(solution)/shard_map/all_gather | solution.py:394
  8.6 8.5 %copy-start.46 = (f32[256]{0:T(256)}, f32[256]{0:T(256)S(1)}, u32[]{:S(2)}) copy-start(f32[256]{0:T(256)S(1)} %broadcast_multiply_fusion.7) | copy-start | bytes 3076
  12.1 95.2 %all-gather.7.cloned.1.call-start = ((), (), s32[]{:S(2)}) async-start(), calls=%async_computation.5 | async-start | bytes 2621440 | tf_op jit(solution)/shard_map/all_gather | solution.py:396
  13.8 138.8 %reduce-scatter.5.cloned.1.call-start = ((), (), s32[]{:S(2)}) async-start(), calls=%async_computation.6 | async-start | bytes 2621440 | tf_op jit(solution)/shard_map/reduce_scatter | solution.py:410
  18.4 249.8 %copy-start.19 = (f32[1024,64]{0,1:T(8,128)}, f32[1024,64]{0,1:T(8,128)S(1)}, u32[]{:S(2)}) copy-start(f32[1024,64]{0,1:T(8,128)S(1)} %get-tuple-element.328) | copy-start | bytes 786436
  89.0 18.3 %copy-start.3 = (bf16[1024,4,64]{0,2,1:T(8,128)(2,1)}, bf16[1024,4,64]{0,2,1:T(8,128)(2,1)S(1)}, u32[]{:S(2)}) copy-start(bf16[1024,4,64]{0,2,1:T(8,128)(2,1)S(1)} %get-tuple-element.566) | copy-start | bytes 1572868
  94.8 60.8 %copy-start.45 = (f32[1024]{0:T(1024)S(1)}, f32[1024]{0:T(1024)}, u32[]{:S(2)}) copy-start(f32[1024]{0:T(1024)} %param.16) | copy-start | bytes 12292
  107.3 95.5 %all-gather.9.cloned.1.call-start = ((), (), s32[]{:S(2)}) async-start(), calls=%async_computation.7 | async-start | bytes 2621440 | tf_op jit(solution)/shard_map/all_gather | solution.py:418
  157.8 105.9 %reduce-scatter.7.cloned.1.call-start = ((), (), s32[]{:S(2)}) async-start(), calls=%async_computation.8 | async-start | bytes 2621440 | tf_op jit(solution)/shard_map/reduce_scatter | solution.py:438
  221.2 97.5 %all-gather.11.cloned.1.call-start = ((), (), s32[]{:S(2)}) async-start(), calls=%async_computation.9 | async-start | bytes 2621440 | tf_op jit(solution)/shard_map/all_gather | solution.py:458
  225.1 25.2 %copy-start.53 = (bf16[656,1024]{1,0:T(8,128)(2,1)S(1)}, bf16[656,1024]{1,0:T(8,128)(2,1)}, u32[]{:S(2)}) copy-start(bf16[656,1024]{1,0:T(8,128)(2,1)} %param.20) | copy-start | bytes 4030468
  225.1 25.2 %copy-start.56 = (bf16[1024,656]{0,1:T(8,128)(2,1)S(1)}, bf16[1024,656]{0,1:T(8,128)(2,1)}, u32[]{:S(2)}) copy-start(bf16[1024,656]{0,1:T(8,128)(2,1)} %get-tuple-element.303) | copy-start | bytes 4030468
  253.5 10.3 %copy-start.9 = (bf16[1,256,1024]{2,1,0:T(8,128)(2,1)S(1)}, bf16[1,256,1024]{2,1,0:T(8,128)(2,1)}, u32[]{:S(2)}) copy-start(bf16[1,256,1024]{2,1,0:T(8,128)(2,1)} %param.13) | copy-start | bytes 1572868
  253.5 10.3 %copy-start.12 = (bf16[256,1024]{1,0:T(8,128)(2,1)S(1)}, bf16[256,1024]{1,0:T(8,128)(2,1)}, u32[]{:S(2)}) copy-start(bf16[256,1024]{1,0:T(8,128)(2,1)} %reduce-scatter.5.cloned.1.call-done) | copy-start | bytes 1572868
  253.5 11.9 %copy-start.30 = (bf16[1,256,1024]{2,1,0:T(8,128)(2,1)S(1)}, bf16[1,256,1024]{2,1,0:T(8,128)(2,1)}, u32[]{:S(2)}) copy-start(bf16[1,256,1024]{2,1,0:T(8,128)(2,1)} %param.21) | copy-start | bytes 1572868
  268.2 116.3 %reduce-scatter.9.cloned.1.call-start = ((), (), s32[]{:S(2)}) async-start(), calls=%async_computation.10 | async-start | bytes 2621440 | tf_op jit(solution)/shard_map/reduce_scatter | solution.py:459
  278.7 38.0 %copy-start.16 = (bf16[1024,656]{0,1:T(8,128)(2,1)S(1)}, bf16[1024,656]{0,1:T(8,128)(2,1)}, u32[]{:S(2)}) copy-start(bf16[1024,656]{0,1:T(8,128)(2,1)} %copy.51) | copy-start | bytes 4030468
  318.5 124.9 %reduce-scatter.11.cloned.1.call-start = ((), (), s32[]{:S(2)}) async-start(), calls=%async_computation.11 | async-start | bytes 2621440 | tf_op jit(solution)/shard_map/reduce_scatter | solution.py:482
  374.5 5.5 %copy-start.33 = (bf16[1024,1,256]{2,0,1:T(8,128)(2,1)S(1)}, bf16[1024,1,256]{2,0,1:T(8,128)(2,1)}, u32[]{:S(2)}) copy-start(bf16[1024,1,256]{2,0,1:T(8,128)(2,1)} %copy.59) | copy-start | bytes 1572868
  391.2 11.8 %copy-start.15 = (bf16[1024,3,256]{2,0,1:T(8,128)(2,1)S(1)}, bf16[1024,3,256]{2,0,1:T(8,128)(2,1)}, u32[]{:S(2)}) copy-start(bf16[1024,3,256]{2,0,1:T(8,128)(2,1)} %pad_maximum_fusion.1) | copy-start | bytes 4718596
  445.5 6.3 %copy-start.1 = (bf16[1024,2,656]{0,2,1:T(8,128)(2,1)S(1)}, bf16[1024,2,656]{0,2,1:T(8,128)(2,1)}, u32[]{:S(2)}) copy-start(bf16[1024,2,656]{0,2,1:T(8,128)(2,1)} %param.19) | copy-start | bytes 8060932
  (53 other events, 143.8 us)
Sparse Core Ops, SparseCore 0:
  12.2 48.3 all-gather.4
  62.8 44.4 all-gather.6
  110.2 42.4 reduce-scatter.4
  157.9 44.8 all-gather.8
  221.3 42.4 reduce-scatter.6
  268.3 44.8 all-gather.10
  318.7 41.9 reduce-scatter.8
  384.6 42.1 reduce-scatter.10

commit v3 on v2

--- a/solution.py
+++ b/solution.py
@@ -52,7 +52,7 @@
     angles = positions.astype(jnp.float32)[:, None] * inv_freq[None, :]
     cos_tab = jnp.concatenate([jnp.cos(angles), jnp.cos(angles)], axis=-1)
     sin_tab = jnp.concatenate([jnp.sin(angles), jnp.sin(angles)], axis=-1)
-    return (cos_tab[:, None, :], sin_tab[:, None, :])
+    return (cos_tab[None], sin_tab[None])
 
 
 def rope_apply(field_in, cos_tab, sin_tab):
@@ -74,85 +74,49 @@
     )
 
 
+def masked_scores(queries, key_rows, seg_row):
+    scale_val = 1.0 / math.sqrt(queries.shape[2])
+    scores = jnp.einsum("hqd,hkd->hqk", queries, key_rows, preferred_element_type=jnp.float32)
+    same_doc = seg_row[:, None] == seg_row[None, :]
+    return jnp.where(same_doc[None], scores * scale_val, neg_fill)
+
+
 def attend_fwd(queries, key_rows, value_rows, seg_row):
-    total_rows = queries.shape[0]
-    block_rows = min(512, total_rows)
-    scale_val = 1.0 / math.sqrt(queries.shape[2])
-
-    def one_block(block_idx):
-        start_row = block_idx * block_rows
-        query_blk = lax.dynamic_slice_in_dim(queries, start_row, block_rows, 0)
-        seg_blk = lax.dynamic_slice_in_dim(seg_row, start_row, block_rows, 0)
-        scores = (
-            jnp.einsum("qhd,khd->hqk", query_blk, key_rows, preferred_element_type=jnp.float32)
-            * scale_val
-        )
-        same_doc = seg_blk[:, None] == seg_row[None, :]
-        scores = jnp.where(same_doc[None], scores, neg_fill)
-        row_top = jnp.max(scores, axis=-1, keepdims=True)
-        exp_vals = jnp.exp(scores - row_top)
-        row_total = jnp.sum(exp_vals, axis=-1, keepdims=True)
-        prob_bf = (exp_vals / row_total).astype(jnp.bfloat16)
-        out_blk = jnp.einsum(
-            "hqk,khd->qhd", prob_bf, value_rows, preferred_element_type=jnp.float32
-        ).astype(jnp.bfloat16)
-        return (out_blk, (row_top + jnp.log(row_total))[..., 0])
-
-    out_blocks, lse_blocks = lax.map(
-        one_block, jnp.arange(total_rows // block_rows, dtype=jnp.int32)
-    )
-    head_count = queries.shape[1]
-    att_out = out_blocks.reshape(total_rows, head_count, queries.shape[2])
-    lse_rows = jnp.transpose(lse_blocks, (1, 0, 2)).reshape(head_count, total_rows)
-    return (att_out, lse_rows)
+    scores = masked_scores(queries, key_rows, seg_row)
+    row_top = jnp.max(scores, axis=-1, keepdims=True)
+    exp_vals = jnp.exp(scores - row_top)
+    row_total = jnp.sum(exp_vals, axis=-1, keepdims=True)
+    prob_bf = (exp_vals / row_total).astype(jnp.bfloat16)
+    att_out = jnp.einsum(
+        "hqk,hkd->hqd", prob_bf, value_rows, preferred_element_type=jnp.float32
+    ).astype(jnp.bfloat16)
+    return (att_out, (row_top + jnp.log(row_total))[..., 0])
 
 
 def attend_bwd(queries, key_rows, value_rows, seg_row, att_out, grad_att, lse_rows):
-    total_rows = queries.shape[0]
-    block_rows = min(512, total_rows)
     scale_val = 1.0 / math.sqrt(queries.shape[2])
     delta_rows = jnp.sum(grad_att.astype(jnp.float32) * att_out.astype(jnp.float32), axis=-1)
-
-    def one_block(acc_pair, block_idx):
-        grad_key, grad_value = acc_pair
-        start_row = block_idx * block_rows
-        query_blk = lax.dynamic_slice_in_dim(queries, start_row, block_rows, 0)
-        grad_blk = lax.dynamic_slice_in_dim(grad_att, start_row, block_rows, 0)
-        seg_blk = lax.dynamic_slice_in_dim(seg_row, start_row, block_rows, 0)
-        delta_blk = lax.dynamic_slice_in_dim(delta_rows, start_row, block_rows, 0)
-        lse_blk = lax.dynamic_slice_in_dim(lse_rows, start_row, block_rows, 1)
-        scores = (
-            jnp.einsum("qhd,khd->hqk", query_blk, key_rows, preferred_element_type=jnp.float32)
-            * scale_val
-        )
-        same_doc = seg_blk[:, None] == seg_row[None, :]
-        scores = jnp.where(same_doc[None], scores, neg_fill)
-        prob_f = jnp.exp(scores - lse_blk[:, :, None])
-        grad_prob = jnp.einsum(
-            "qhd,khd->hqk", grad_blk, value_rows, preferred_element_type=jnp.float32
-        )
-        grad_score = prob_f * (grad_prob - jnp.transpose(delta_blk)[:, :, None])
-        prob_bf = prob_f.astype(jnp.bfloat16)
-        score_bf = grad_score.astype(jnp.bfloat16)
-        grad_value = grad_value + jnp.einsum(
-            "hqk,qhd->khd", prob_bf, grad_blk, preferred_element_type=jnp.float32
-        )
-        grad_key = (
-            grad_key
-            + jnp.einsum("hqk,qhd->khd", score_bf, query_blk, preferred_element_type=jnp.float32)
-            * scale_val
-        )
-        grad_query_blk = (
-            jnp.einsum("hqk,khd->qhd", score_bf, key_rows, preferred_element_type=jnp.float32)
-            * scale_val
-        )
-        return ((grad_key, grad_value), grad_query_blk)
-
-    zero_rows = jnp.zeros(key_rows.shape, jnp.float32)
-    acc_pair, query_blocks = lax.scan(
-        one_block, (zero_rows, zero_rows), jnp.arange(total_rows // block_rows, dtype=jnp.int32)
-    )
-    return (query_blocks.reshape(queries.shape), acc_pair[0], acc_pair[1])
+    scores = masked_scores(queries, key_rows, seg_row)
+    prob_f = jnp.exp(scores - lse_rows[:, :, None])
+    grad_prob = jnp.einsum("hqd,hkd->hqk", grad_att, value_rows, preferred_element_type=jnp.float32)
+    score_bf = (prob_f * (grad_prob - delta_rows[:, :, None])).astype(jnp.bfloat16)
+    prob_bf = prob_f.astype(jnp.bfloat16)
+    grad_value = jnp.einsum("hqk,hqd->hkd", prob_bf, grad_att, preferred_element_type=jnp.float32)
+    grad_key = (
+        jnp.einsum("hqk,hqd->hkd", score_bf, queries, preferred_element_type=jnp.float32) * scale_val
+    )
+    grad_query = (
+        jnp.einsum("hqk,hkd->hqd", score_bf, key_rows, preferred_element_type=jnp.float32) * scale_val
+    )
+    return (grad_query, grad_key, grad_value)
+
+
+def heads_first(field_in, head_local):
+    return jnp.transpose(field_in.reshape(field_in.shape[0], head_local, HEAD_DIM), (1, 0, 2))
+
+
+def rows_first(field_in):
+    return jnp.transpose(field_in, (1, 0, 2)).reshape(field_in.shape[1], -1)
 
 
 def bit_orders(n_dp):
@@ -399,12 +363,15 @@
         w_qkv.reshape(model_width, 3 * width_local),
         preferred_element_type=jnp.float32,
     )
-    projected = projected.reshape(total_rows, 3, head_local, HEAD_DIM)
-    queries = rope_apply(projected[:, 0], cos_tab, sin_tab).astype(jnp.bfloat16)
-    key_rows = rope_apply(projected[:, 1], cos_tab, sin_tab).astype(jnp.bfloat16)
-    value_rows = projected[:, 2].astype(jnp.bfloat16)
+    query_f, key_f, value_f = (
+        heads_first(projected[:, i * width_local : (i + 1) * width_local], head_local)
+        for i in range(3)
+    )
+    queries = rope_apply(query_f, cos_tab, sin_tab).astype(jnp.bfloat16)
+    key_rows = rope_apply(key_f, cos_tab, sin_tab).astype(jnp.bfloat16)
+    value_rows = value_f.astype(jnp.bfloat16)
     att_out, lse_rows = attend_fwd(queries, key_rows, value_rows, seg_row)
-    att_flat = att_out.reshape(total_rows, width_local)
+    att_flat = rows_first(att_out)
     att_part = jnp.dot(att_flat, w_out, preferred_element_type=jnp.float32).astype(jnp.bfloat16)
     att_part, grad_all = lax.optimization_barrier((att_part, grad_all))
     att_sum = lax.psum_scatter(
@@ -463,44 +430,46 @@
     d_att = lax.dot_general(
         d_mid_all, w_out, (((1,), (1,)), ((), ())), preferred_element_type=jnp.float32
     )
-    d_att = d_att.astype(jnp.bfloat16).reshape(total_rows, head_local, HEAD_DIM)
+    d_att = heads_first(d_att.astype(jnp.bfloat16), head_local)
     grad_query, grad_key, grad_value = attend_bwd(
         queries, key_rows, value_rows, seg_row, att_out, d_att, lse_rows
     )
     grad_query = rope_back(grad_query, cos_tab, sin_tab)
     grad_key = rope_back(grad_key, cos_tab, sin_tab)
-    d_proj = (
-        jnp.stack([grad_query, grad_key, grad_value], axis=1)
-        .reshape(total_rows, 3, width_local)
-        .astype(jnp.bfloat16)
+    d_proj = jnp.concatenate(
+        [rows_first(g.astype(jnp.bfloat16)) for g in (grad_query, grad_key, grad_value)], axis=1
     )
     d_attn_part = lax.dot_general(
-        d_proj, w_qkv, (((1, 2), (1, 2)), ((), ())), preferred_element_type=jnp.float32
+        d_proj,
+        w_qkv.reshape(model_width, 3 * width_local),
+        (((1,), (1,)), ((), ())),
+        preferred_element_type=jnp.float32,
     ).astype(jnp.bfloat16)
-    d_attn_part, mlp_sum, d_proj = lax.optimization_barrier((d_attn_part, mlp_sum, d_proj))
+    grad_out_w = lax.dot_general(
+        d_mid_all, att_flat, (((0,), (0,)), ((), ())), preferred_element_type=jnp.float32
+    )
+    (grad_out_w,) = grad_reduce([grad_out_w], 4)
+    grad_out_w = jnp.transpose(grad_out_w.astype(jnp.float32))
+    grad_in = grad_in.astype(jnp.float32).reshape(model_width, 2, ff_local)
+    d_attn_part, mlp_sum, d_proj, grad_out_w, grad_in = lax.optimization_barrier(
+        (d_attn_part, mlp_sum, d_proj, grad_out_w, grad_in)
+    )
     final_rows = (mid_rows + mlp_sum.astype(jnp.float32)).astype(jnp.bfloat16)
     d_norm_attn = lax.psum_scatter(d_attn_part, "tensor", scatter_dimension=0, tiled=True)
     grad_qkv = lax.dot_general(
         gathered_attn,
-        d_proj.reshape(total_rows, 3 * width_local),
+        d_proj,
         (((0,), (0,)), ((), ())),
         preferred_element_type=jnp.float32,
-    )
-    grad_out_w = lax.dot_general(
-        d_mid_all, att_flat, (((0,), (0,)), ((), ())), preferred_element_type=jnp.float32
     )
     gain_attn_part = (
         jnp.sum(d_attn_part.astype(jnp.float32) * gathered_attn.astype(jnp.float32), axis=0)
         / gain_attn
     )
     gain_both = gain_reduce(jnp.stack([gain_attn_part, gain_mlp_part]), 3)
-    grad_qkv, grad_out_w = grad_reduce([grad_qkv, grad_out_w], 1)
+    (grad_qkv,) = grad_reduce([grad_qkv], 1)
     grad_qkv = grad_qkv.astype(jnp.float32).reshape(model_width, 3, width_local)
-    grad_in = grad_in.astype(jnp.float32).reshape(model_width, 2, ff_local)
-    grad_out_w = jnp.transpose(grad_out_w.astype(jnp.float32))
-    d_norm_attn, gain_both, grad_qkv, grad_out_w, grad_in = lax.optimization_barrier(
-        (d_norm_attn, gain_both, grad_qkv, grad_out_w, grad_in)
-    )
+    d_norm_attn, gain_both, grad_qkv = lax.optimization_barrier((d_norm_attn, gain_both, grad_qkv))
     d_norm_attn = d_norm_attn.astype(jnp.float32)
     d_rows = d_mid + norm_bwd(d_norm_attn, hat_attn, inv_attn, gain_attn)
     return (

time: 464 us -> 446 us (0.961)
  local copies, waits for them, and re-layouts: 55.1 us -> 39.1 us
  Pallas kernels: 103 us -> 115 us
  loops' own time: 11.7 us -> 0 us
    another operation x2 -> x0, loops' own time: 11.7 us -> none  [the longest x1 10.2 us: attend_bwd(): lax.scan(one_block, (zero_rows, zero_rows), jnp.arange(total_rows // bloc...]
    pallas_call x3 -> x4, Pallas kernels: 93.2 us -> 104 us  [grad_reduce(): pl.pallas_call(functools.partial(grad_reduce_kernel, n_dp, n_arr), out_sh...]
    reshape x1, local copies, waits for them, and re-layouts: 3.47 us -> 11.7 us  [shards(): grad_in = grad_in.astype(jnp.float32).reshape(model_width, 2, ff_local)]
    reshape x3 -> x0, local copies, waits for them, and re-layouts: 7.4 us -> none  [attend_bwd(): return (query_blocks.reshape(queries.shape), acc_pair[0], acc_pair[1])]
    another operation x4 -> x0, other arithmetic: 5.91 us -> none
    while x49 -> x0, local copies, waits for them, and re-layouts: 5.87 us -> none
    dot_general x16 -> x8, matrix products: 39.6 us -> 44.5 us  [the longest x1 9.82 us: attend_bwd(): jnp.einsum('hqd,hkd->hqk', grad_att, value_rows, preferred_element_type=j...]
    unnamed x93 -> x94, local copies, waits for them, and re-layouts: 13 us -> 14.2 us
  transfers between devices with their start and end apart: 8 -> 8, of which waited for: 5 -> 5; matrix products, arithmetic and copies ran while one was open for 29% -> 26% of each run, Pallas kernels for 23% -> 26%
where the time goes in v3:
time: 446 us; the launch traced here: 441 us
  waiting for transfers between devices  149 us (33%)
  Pallas kernels  115 us (26%)
  matrix products  81.1 us (18%)
  other arithmetic  42 us (9%)
  local copies, waits for them, and re-layouts  39.1 us (9%)
  between operations  15 us (3%)
    pallas_call x4, Pallas kernels, grad_reduce(): pl.pallas_call(functools.partial(grad_reduce_kernel, n_dp, n_arr), out_sh...  104 us
    reduce_scatter x1, waiting for transfers between devices, shards(): lax.psum_scatter(att_part, 'tensor', scatter_dimension=0, tiled=True)  45 us
    all_gather x1, waiting for transfers between devices, shards(): gathered_mlp = lax.all_gather(normed_mlp, 'tensor', axis=0, tiled=True)  45 us
    all_gather x1, waiting for transfers between devices, shards(): gathered_attn = lax.all_gather(normed_attn, 'tensor', axis=0, tiled=True)  40.6 us
    all_gather x1, waiting for transfers between devices, shards(): lax.all_gather(grad_top.astype(jnp.bfloat16), 'tensor', axis=0, tiled=True)  15.1 us
    unnamed x94, local copies, waits for them, and re-layouts  14.2 us
    reshape x1, local copies, waits for them, and re-layouts, shards(): grad_in = grad_in.astype(jnp.float32).reshape(model_width, 2, ff_local)  11.7 us
    pallas_call x1, Pallas kernels, gain_reduce(): pl.pallas_call(functools.partial(gain_reduce_kernel, n_dp, n_tp), out_sha...  10.4 us
  transfers between devices with their start and end apart: 8, of which 5 were waited for; matrix products, arithmetic and copies ran while one was open for 26% of the time, Pallas kernels for 26%

profile of v3, /device:TPU:0, one launch (start us, length us, event | category | flops | bytes accessed | tf_op | source)
XLA Modules:
  0.0 441.4 jit_solution(3259426327985450053)
XLA Ops:
  20.0 40.6 %all-gather.5.cloned.1.call-done = bf16[1024,1024]{1,0:T(8,128)(2,1)} async-done(((bf16[256,1024]{1,0:T(8,128)(2,1)}), bf16[1024,1024]{1,0:T(8,128)(2,1)}) %all-gather.5.cloned.1.call-update) | async-done | bytes 2097168 | tf_op jit(solution)/shard_map/all_gather | solution.py:358
  60.6 3.9 fusion.58
  66.2 7.6 %fusion.57 = (f32[4,1024]{1,0:T(4,128)S(1)}, f32[4,1024,1024]{1,2,0:T(8,128)}) fusion(bf16[4,1024,64]{1,2,0:T(8,128)(2,1)S(1)} %get-tuple-element.95, bf16[4,1024,64]{1,2,0:T(8,128)(2,1)S(1)} %get-tuple-element.94, pred[1024,1024]{0,1:T(8,128)(4,1)S(1)} %copy-done.7), kind=kOutput, calls=%fused_computation.122 | convolution fusion | flops 549449728 | bytes 18890752 | tf_op jit(solution)/shard_map/hqd,hkd->hqk/dot_general | solution.py:79
  73.7 8.0 %fusion = f32[4,1024]{1,0:T(4,128)S(1)} fusion(f32[4,1024,1024]{1,2,0:T(8,128)} %get-tuple-element.109, f32[4,1024]{1,0:T(4,128)S(1)} %get-tuple-element.108), kind=kLoop, calls=%fused_computation.5 | loop fusion | flops 8384512 | bytes 16809984 | tf_op jit(solution)/shard_map/reduce_sum | solution.py:88
  81.8 7.5 %fusion.25 = bf16[4,1024,64]{1,2,0:T(8,128)(2,1)S(1)} fusion(bf16[4,1024,64]{1,2,0:T(8,128)(2,1)S(1)} %bitcast.196, f32[4,1024,1024]{1,2,0:T(8,128)} %get-tuple-element.109, f32[4,1024]{1,0:T(4,128)S(1)} %fusion, f32[4,1024]{1,0:T(4,128)S(1)} %get-tuple-element.108), kind=kOutput, calls=%fused_computation.53 | convolution fusion | flops 549715968 | bytes 17858560 | tf_op jit(solution)/shard_map/hqk,hkd->hqd/dot_general | solution.py:90
  92.2 15.1 %all-gather.7.cloned.1.call-done = bf16[1024,1024]{1,0:T(8,128)(2,1)} async-done(((bf16[256,1024]{1,0:T(8,128)(2,1)}), bf16[1024,1024]{1,0:T(8,128)(2,1)}) %all-gather.7.cloned.1.call-update) | async-done | bytes 2097168 | tf_op jit(solution)/shard_map/all_gather | solution.py:360
  107.6 45.0 %reduce-scatter.5.cloned.1.call-done = bf16[256,1024]{1,0:T(8,128)(2,1)} async-done(((bf16[1024,1024]{1,0:T(8,128)(2,1)}), bf16[256,1024]{1,0:T(8,128)(2,1)}) %reduce-scatter.5.cloned.1.call-update) | async-done | bytes 524304 | tf_op jit(solution)/shard_map/reduce_scatter | solution.py:377
  157.4 45.0 %all-gather.9.cloned.1.call-done = bf16[1024,1024]{1,0:T(8,128)(2,1)} async-done(((bf16[256,1024]{1,0:T(8,128)(2,1)}), bf16[1024,1024]{1,0:T(8,128)(2,1)}) %all-gather.9.cloned.1.call-update) | async-done | bytes 2097168 | tf_op jit(solution)/shard_map/all_gather | solution.py:385
  202.4 4.7 %fusion.12 = f32[1024,2,656]{0,2,1:T(8,128)S(1)} fusion(bf16[1024,2,656]{0,2,1:T(8,128)(2,1)S(1)} %copy-done, bf16[1024,1024]{1,0:T(8,128)(2,1)} %all-gather.9.cloned.1.call-done), kind=kOutput, calls=%fused_computation.24 | convolution fusion | flops 2751463424 | bytes 10158080 | tf_op jit(solution)/shard_map/dot_general | solution.py:386
  207.1 3.8 fusion.16
  212.5 4.6 %bitcast_convert_fusion = bf16[1024,1024]{1,0:T(8,128)(2,1)} fusion(bf16[1024,2,656]{0,2,1:T(8,128)(2,1)S(1)} %copy-done, bf16[1024,1,656]{0,2,1:T(8,128)(2,1)S(1)} %get-tuple-element.80, bf16[1024,1,656]{0,2,1:T(8,128)(2,1)S(1)} %get-tuple-element.79), kind=kOutput, calls=%fused_computation.10 | convolution fusion | flops 2753855488 | bytes 7471104 | tf_op jit(solution)/shard_map/dot_general | solution.py:401
  217.2 3.6 pad_maximum_fusion
  224.7 25.2 %shard_map.152 = bf16[2,8,64,656]{3,2,1,0:T(8,128)(2,1)S(1)} custom-call(bf16[2,8,64,656]{3,2,1,0:T(8,128)(2,1)S(1)} %bitcast.185), custom_call_target="tpu_custom_call" | custom-call | bytes 40304640 | tf_op jit(solution)/shard_map/pallas_call | solution.py:247
  253.1 7.0 %convolution_convert_fusion = bf16[1024,1312]{0,1:T(8,128)(2,1)} fusion(bf16[1024,1312]{0,1:T(8,128)(2,1)} %bitcast.193, bf16[1024,1024]{1,0:T(8,128)(2,1)} %all-gather.9.cloned.1.call-done), kind=kOutput, calls=%fused_computation.14 | convolution fusion | flops 2752806912 | bytes 7471104 | tf_op jit(solution)/shard_map/dot_general | solution.py:410
  269.3 4.5 %copy.31 = bf16[1024,1312]{1,0:T(8,128)(2,1)} copy(bf16[1024,1312]{0,1:T(8,128)(2,1)} %convolution_convert_fusion) | data formatting | bytes 5373952 | tf_op jit(solution)/shard_map/optimization_barrier | solution.py:422
  275.8 38.0 %shard_map.153 = bf16[2,8,64,1312]{3,2,1,0:T(8,128)(2,1)S(1)} custom-call(bf16[2,8,64,1312]{3,2,1,0:T(8,128)(2,1)S(1)} %bitcast.183), custom_call_target="tpu_custom_call" | custom-call | bytes 80609280 | tf_op jit(solution)/shard_map/pallas_call | solution.py:247
  320.0 16.9 %shard_map.154 = bf16[2,8,64,256]{3,2,1,0:T(8,128)(2,1)S(1)} custom-call(bf16[2,8,64,256]{3,2,1,0:T(8,128)(2,1)S(1)} %bitcast.187), custom_call_target="tpu_custom_call" | custom-call | bytes 15728640 | tf_op jit(solution)/shard_map/pallas_call | solution.py:247
  340.6 11.7 %copy.38 = f32[1024,1312]{0,1:T(8,128)} copy(bf16[1024,1312]{1,0:T(8,128)(2,1)S(1)} %bitcast.182) | data formatting | bytes 8060928 | tf_op jit(solution)/shard_map/reshape | solution.py:453
  352.3 9.8 %multiply_convert_fusion = bf16[4,1024,1024]{1,2,0:T(8,128)(2,1)S(1)} fusion(f32[4,1024,1024]{1,2,0:T(8,128)} %get-tuple-element.109, bf16[4,1024,64]{1,2,0:T(8,128)(2,1)} %bitcast.194, bf16[4,1024,64]{1,2,0:T(8,128)(2,1)} %bitcast.197, f32[4,1024]{1,0:T(4,128)S(1)} %get-tuple-element.110, f32[4,1024]{1,0:T(4,128)S(1)} %log_add_fusion), kind=kOutput, calls=%fused_computation | convolution fusion | flops 553648128 | bytes 26247168 | tf_op jit(solution)/shard_map/hqd,hkd->hqk/dot_general | solution.py:101
  369.0 8.5 %fusion.22 = bf16[4,1024,64]{1,2,0:T(8,128)(2,1)S(1)} fusion(bf16[4,1024,64]{1,2,0:T(8,128)(2,1)S(1)} %bitcast.195, f32[4,1024,1024]{1,2,0:T(8,128)} %get-tuple-element.109, f32[4,1024]{1,0:T(4,128)S(1)} %log_add_fusion), kind=kOutput, calls=%fused_computation.50 | convolution fusion | flops 545521664 | bytes 17842176 | tf_op jit(solution)/shard_map/hqk,hqd->hkd/dot_general | solution.py:104
  383.1 3.6 convolution_convert_fusion.4
  386.7 24.1 %shard_map.156 = bf16[2,8,64,768]{3,2,1,0:T(8,128)(2,1)S(1)} custom-call(bf16[2,8,64,768]{3,2,1,0:T(8,128)(2,1)S(1)} %bitcast.186), custom_call_target="tpu_custom_call" | custom-call | bytes 47185920 | tf_op jit(solution)/shard_map/pallas_call | solution.py:247
  412.5 10.4 %shard_map.155 = f32[2,256]{1,0:T(2,128)} custom-call(f32[4,2,256]{2,1,0:T(2,128)} %maximum_bitcast_fusion.x_ref), custom_call_target="tpu_custom_call" | custom-call | bytes 20971520 | tf_op jit(solution)/shard_map/pallas_call | solution.py:321
  428.1 4.6 %copy.39 = f32[1024,3,256]{2,0,1:T(8,128)} copy(f32[1024,3,256]{2,1,0:T(4,128)} %reshape.221) | data formatting | bytes 6291456
  (166 shorter events, 72.6 us)
Async XLA Ops:
  7.2 195.2 %copy-start = (bf16[1024,2,656]{0,2,1:T(8,128)(2,1)S(1)}, bf16[1024,2,656]{0,2,1:T(8,128)(2,1)}, u32[]{:S(2)}) copy-start(bf16[1024,2,656]{0,2,1:T(8,128)(2,1)} %param.15) | copy-start | bytes 8060932
  7.2 53.4 %all-gather.5.cloned.1.call-start = ((), (), s32[]{:S(2)}) async-start(), calls=%async_computation.4 | async-start | bytes 2621440 | tf_op jit(solution)/shard_map/all_gather | solution.py:358
  12.1 95.2 %all-gather.7.cloned.1.call-start = ((), (), s32[]{:S(2)}) async-start(), calls=%async_computation.5 | async-start | bytes 2621440 | tf_op jit(solution)/shard_map/all_gather | solution.py:360
  13.8 138.8 %reduce-scatter.5.cloned.1.call-start = ((), (), s32[]{:S(2)}) async-start(), calls=%async_computation.6 | async-start | bytes 2621440 | tf_op jit(solution)/shard_map/reduce_scatter | solution.py:377
  64.6 17.2 %copy-start.19 = (bf16[1024,256]{0,1:T(8,128)(2,1)}, bf16[1024,256]{0,1:T(8,128)(2,1)S(1)}, u32[]{:S(2)}) copy-start(bf16[1024,256]{0,1:T(8,128)(2,1)S(1)} %slice.105) | copy-start | bytes 1572868
  81.8 8.3 %copy-start.32 = (bf16[256,1024]{1,0:T(8,128)(2,1)S(1)}, bf16[256,1024]{1,0:T(8,128)(2,1)}, u32[]{:S(2)}) copy-start(bf16[256,1024]{1,0:T(8,128)(2,1)} %param.14) | copy-start | bytes 1572868
  89.3 63.3 %copy-start.3 = (bf16[1,256,1024]{2,1,0:T(8,128)(2,1)S(1)}, bf16[1,256,1024]{2,1,0:T(8,128)(2,1)}, u32[]{:S(2)}) copy-start(bf16[1,256,1024]{2,1,0:T(8,128)(2,1)} %param.9) | copy-start | bytes 1572868
  92.2 63.0 %copy-start.38 = (f32[1024]{0:T(1024)S(1)}, f32[1024]{0:T(1024)}, u32[]{:S(2)}) copy-start(f32[1024]{0:T(1024)} %param.12) | copy-start | bytes 12292
  107.3 95.0 %all-gather.9.cloned.1.call-start = ((), (), s32[]{:S(2)}) async-start(), calls=%async_computation.7 | async-start | bytes 2621440 | tf_op jit(solution)/shard_map/all_gather | solution.py:385
  157.3 106.1 %reduce-scatter.7.cloned.1.call-start = ((), (), s32[]{:S(2)}) async-start(), calls=%async_computation.8 | async-start | bytes 2621440 | tf_op jit(solution)/shard_map/reduce_scatter | solution.py:405
  220.8 95.0 %all-gather.11.cloned.1.call-start = ((), (), s32[]{:S(2)}) async-start(), calls=%async_computation.9 | async-start | bytes 2621440 | tf_op jit(solution)/shard_map/all_gather | solution.py:425
  224.7 25.2 %copy-start.43 = (bf16[656,1024]{1,0:T(8,128)(2,1)S(1)}, bf16[656,1024]{1,0:T(8,128)(2,1)}, u32[]{:S(2)}) copy-start(bf16[656,1024]{1,0:T(8,128)(2,1)} %param.16) | copy-start | bytes 4030468
  224.7 25.2 %copy-start.45 = (bf16[1024,656]{0,1:T(8,128)(2,1)S(1)}, bf16[1024,656]{0,1:T(8,128)(2,1)}, u32[]{:S(2)}) copy-start(bf16[1024,656]{0,1:T(8,128)(2,1)} %get-tuple-element.81) | copy-start | bytes 4030468
  253.1 10.3 %copy-start.4 = (bf16[1,256,1024]{2,1,0:T(8,128)(2,1)S(1)}, bf16[1,256,1024]{2,1,0:T(8,128)(2,1)}, u32[]{:S(2)}) copy-start(bf16[1,256,1024]{2,1,0:T(8,128)(2,1)} %param.9) | copy-start | bytes 1572868
  253.1 10.3 %copy-start.5 = (bf16[256,1024]{1,0:T(8,128)(2,1)S(1)}, bf16[256,1024]{1,0:T(8,128)(2,1)}, u32[]{:S(2)}) copy-start(bf16[256,1024]{1,0:T(8,128)(2,1)} %reduce-scatter.5.cloned.1.call-done) | copy-start | bytes 1572868
  253.1 11.9 %copy-start.22 = (bf16[1,256,1024]{2,1,0:T(8,128)(2,1)S(1)}, bf16[1,256,1024]{2,1,0:T(8,128)(2,1)}, u32[]{:S(2)}) copy-start(bf16[1,256,1024]{2,1,0:T(8,128)(2,1)} %param.17) | copy-start | bytes 1572868
  267.8 115.2 %reduce-scatter.9.cloned.1.call-start = ((), (), s32[]{:S(2)}) async-start(), calls=%async_computation.10 | async-start | bytes 2621440 | tf_op jit(solution)/shard_map/reduce_scatter | solution.py:426
  275.8 38.0 %copy-start.13 = (bf16[1024,656]{0,1:T(8,128)(2,1)S(1)}, bf16[1024,656]{0,1:T(8,128)(2,1)}, u32[]{:S(2)}) copy-start(bf16[1024,656]{0,1:T(8,128)(2,1)} %copy.32) | copy-start | bytes 4030468
  315.7 110.4 %reduce-scatter.11.cloned.1.call-start = ((), (), s32[]{:S(2)}) async-start(), calls=%async_computation.11 | async-start | bytes 2621440 | tf_op jit(solution)/shard_map/reduce_scatter | solution.py:458
  352.3 9.8 %copy-start.10 = (bf16[4,1024,64]{1,2,0:T(8,128)(2,1)S(1)}, bf16[4,1024,64]{1,2,0:T(8,128)(2,1)}, u32[]{:S(2)}) copy-start(bf16[4,1024,64]{1,2,0:T(8,128)(2,1)} %copy-done.9) | copy-start | bytes 1572868
  369.0 8.6 %copy-start.23 = (bf16[4,1024,64]{1,2,0:T(8,128)(2,1)S(1)}, bf16[4,1024,64]{1,2,0:T(8,128)(2,1)}, u32[]{:S(2)}) copy-start(bf16[4,1024,64]{1,2,0:T(8,128)(2,1)} %get-tuple-element.96) | copy-start | bytes 1572868
  369.0 8.6 %copy-start.25 = (bf16[4,1024,64]{1,2,0:T(8,128)(2,1)S(1)}, bf16[4,1024,64]{1,2,0:T(8,128)(2,1)}, u32[]{:S(2)}) copy-start(bf16[4,1024,64]{1,2,0:T(8,128)(2,1)} %get-tuple-element.97) | copy-start | bytes 1572868
  383.1 27.8 %copy-start.18 = (bf16[1024,1024]{1,0:T(8,128)(2,1)S(1)}, bf16[1024,1024]{1,0:T(8,128)(2,1)}, u32[]{:S(2)}) copy-start(bf16[1024,1024]{1,0:T(8,128)(2,1)} %all-gather.5.cloned.1.call-done) | copy-start | bytes 6291460
  386.7 24.1 %copy-start.8 = (bf16[1024,1024]{1,0:T(8,128)(2,1)S(1)}, bf16[1024,1024]{1,0:T(8,128)(2,1)}, u32[]{:S(2)}) copy-start(bf16[1024,1024]{1,0:T(8,128)(2,1)} %convolution_convert_fusion.2) | copy-start | bytes 6291460
  (30 other events, 101.9 us)
Sparse Core Ops, SparseCore 0:
  12.2 48.3 all-gather.4
  62.8 44.4 all-gather.6
  110.1 42.4 reduce-scatter.4
  157.5 44.8 all-gather.8
  220.9 42.4 reduce-scatter.6
  267.9 44.8 all-gather.10
  315.8 41.8 reduce-scatter.8
  383.2 41.9 reduce-scatter.10
